TPU v7x, 32 devices: a whole 2x2x4 slice. The times are simulated.
32 devices in a mesh: row: 8 (over z, core), col: 4 (over y, x).
Axes of the slice: x: 2, y: 2, z: 4, core: 2. Of those that a mesh axis runs over, the one named last changes fastest.
Arguments:
- die_current: float32 [16, 1024, 1024], P(None, 'row', 'col')
- die_shunt: float32 [1024, 1024], P('row', 'col'), may hold values from 0.01 to 0.1
- pkg_current: float32 [16, 4096], P(None, ('row', 'col')), may hold values from -6 to 6
- pkg_matrix: float32 [4096, 4096], P('row', 'col'), as said below
- pkg_block_inv: float32 [128, 32, 32], P(('row', 'col')), as said below
- bump_node: int32 [4096], replicated, may hold values from 0 to 1048575, as said below
- bump_conductance: float32 [4096], replicated, may hold values from 0.5 to 4
Outputs:
- die_drop: float32 [16, 1024, 1024], P(None, 'row', 'col')
- package_drop: float32 [16, 4096], P(None, ('row', 'col'))
Inputs may be any that keep to these rules, and one draw needn't show every extreme that they name: `bump_node`: bump b lies in lattice cell (b // 64, b % 64) of the die, the cells being 16 rows by 16 columns; the entry is row * 1024 + column, so no two bumps share a node. `pkg_matrix`: symmetric positive definite. `pkg_block_inv`: each block is symmetric positive definite.
All inputs are finite; a program needn't handle non-finite values.
Results may differ from a plain program's by a relative error of at most 0.0003.
Values sent between devices are 32-bit elements; how exact they have to be, the bound alone decides.
A program may use at most 128 MiB of HBM per device.

v0:
```python
import jax
import jax.numpy as jnp
from jax import lax
from jax.sharding import PartitionSpec as P

BUMP_C = 64
PB = 32
ITERS = 3


def with_halo(block, sides, width):
    for axis, dim in sides:
        count = lax.axis_size(axis)
        forward = [(i, i + 1) for i in range(count - 1)]
        backward = [(target, source) for source, target in forward]
        low = lax.ppermute(
            lax.slice_in_dim(block, block.shape[dim] - width, None, axis=dim), axis, forward
        )
        high = lax.ppermute(lax.slice_in_dim(block, 0, width, axis=dim), axis, backward)
        block = jnp.concatenate([low, block, high], axis=dim)
    return block


def inner(ad, ap, bd, bp):
    return jnp.sum(ad * bd, axis=(1, 2)) + jnp.sum(ap * bp, axis=1)


def body(
    die_current, die_shunt, pkg_current, pkg_matrix, pkg_block_inv, bump_node, bump_conductance
):
    nrows = lax.axis_size("row")
    ncols = lax.axis_size("col")
    irow = lax.axis_index("row")
    icol = lax.axis_index("col")
    batch, tile_r, tile_c = die_current.shape
    total_c = tile_c * ncols
    bumps = bump_node.shape[0]
    local_n = pkg_current.shape[1]
    start = (irow * ncols + icol) * local_n
    lat_rows = bumps // BUMP_C // nrows
    lat_cols = BUMP_C // ncols
    seg_len = bumps // nrows
    cond_here = lax.dynamic_slice_in_dim(bump_conductance, start, local_n)
    step_r = jnp.arange(lat_rows, dtype=jnp.int32)
    step_c = jnp.arange(lat_cols, dtype=jnp.int32)
    chosen = (
        (irow * lat_rows + step_r[:, None]) * BUMP_C + icol * lat_cols + step_c[None, :]
    ).reshape(-1)
    nodes = bump_node[chosen]
    loc_r = nodes // total_c - irow * tile_r
    loc_c = nodes % total_c - icol * tile_c
    inside = (loc_r >= 0) & (loc_r < tile_r) & (loc_c >= 0) & (loc_c < tile_c)
    weight = inside.astype(jnp.float32)
    loc_r = jnp.clip(loc_r, 0, tile_r - 1)
    loc_c = jnp.clip(loc_c, 0, tile_c - 1)
    cond_sel = bump_conductance[chosen] * weight
    seg_index = jnp.clip(chosen - irow * seg_len, 0, seg_len - 1)
    diag_die = (4.0 + die_shunt).at[loc_r, loc_c].add(cond_sel)

    def precond(rd, rp):
        blocks = rp.reshape(batch, -1, PB)
        zp = jnp.einsum("bac,kbc->kba", pkg_block_inv, blocks, precision=lax.Precision.HIGHEST)
        return (rd / diag_die, zp.reshape(batch, local_n))

    xd = jnp.zeros_like(die_current)
    xp = jnp.zeros_like(pkg_current)
    rd, rp = (die_current, pkg_current)

    def norm_sum(ad, ap, bd, bp):
        return lax.psum(inner(ad, ap, bd, bp), ("row", "col"))

    zd, zp = precond(rd, rp)
    pd, pp = (zd, zp)
    rz = norm_sum(rd, rp, zd, zp)
    for step in range(ITERS):
        padded = with_halo(pd, (("row", 1), ("col", 2)), 1)
        beside_all = padded[:, 2:, 1:-1] + padded[:, :-2, 1:-1]
        beside_all = beside_all + padded[:, 1:-1, 2:] + padded[:, 1:-1, :-2]
        die = (4.0 + die_shunt) * pd - beside_all
        segment = lax.all_gather(pp, "col", axis=1, tiled=True)
        partial_value = jnp.dot(segment, pkg_matrix, precision=lax.Precision.HIGHEST)
        pieces = partial_value.reshape(batch, nrows // ncols, ncols, local_n).transpose(0, 2, 1, 3)
        moved = lax.all_to_all(pieces, "col", split_axis=1, concat_axis=1, tiled=True)
        pkg_term = lax.psum_scatter(
            moved.reshape(batch, nrows * local_n), "row", scatter_dimension=1, tiled=True
        )
        pkg_at = jnp.take(segment, seg_index, axis=1)
        at_bumps = pd[:, loc_r, loc_c] * weight
        band = jnp.zeros((batch, lat_rows, BUMP_C), jnp.float32)
        band = lax.dynamic_update_slice(
            band,
            at_bumps.reshape(batch, lat_rows, lat_cols),
            (jnp.int32(0), jnp.int32(0), icol * lat_cols),
        )
        die_at = lax.psum_scatter(
            band.reshape(batch, seg_len), "col", scatter_dimension=1, tiled=True
        )
        die = die.at[:, loc_r, loc_c].add(cond_sel * (at_bumps - pkg_at))
        qp = pkg_term + cond_here * (pp - die_at)
        alpha = rz / lax.psum(inner(pd, pp, die, qp), ("row", "col"))
        xd = xd + alpha[:, None, None] * pd
        xp = xp + alpha[:, None] * pp
        rd = rd - alpha[:, None, None] * die
        rp = rp - alpha[:, None] * qp
        if step + 1 < ITERS:
            zd, zp = precond(rd, rp)
            fresh = norm_sum(rd, rp, zd, zp)
            ratio = fresh / rz
            pd = zd + ratio[:, None, None] * pd
            pp = zp + ratio[:, None] * pp
            rz = fresh
    return (xd, xp)


def solution(mesh):
    placed = (
        P(None, "row", "col"),
        P("row", "col"),
        P(None, ("row", "col")),
        P("row", "col"),
        P(("row", "col"), None, None),
        P(),
        P(),
    )
    return jax.shard_map(
        body,
        mesh=mesh,
        in_specs=placed,
        out_specs=(P(None, "row", "col"), P(None, ("row", "col"))),
        check_vma=False,
    )
```

profile of v0, /device:TPU:0, one launch (start us, length us, event | category | flops | bytes accessed | tf_op | source)
XLA Modules:
  0.0 648.6 jit_solution(8690379113973519526)
XLA Ops:
  7.4 1.8 gather_fusion
  9.8 1.6 gather_fusion.1
  12.4 7.2 %scatter_fusion = f32[128,256]{1,0:T(8,128)S(1)} fusion(f32[128,256]{1,0:T(8,128)S(1)} %copy.371, s32[128]{0:T(128)S(1)} %get-tuple-element.38, f32[128]{0:T(128)S(1)} %broadcast_select_fusion), kind=kCustom, calls=%fused_computation.8 | custom fusion | flops 128 | bytes 2560 | tf_op jit(solution)/shard_map/scatter-add | solution.py:58
  19.6 1.8 broadcast_divide_fusion
  24.1 3.2 collective-permute-start.1
  27.3 9.9 %copy.324 = f32[16,128,256]{0,2,1:T(8,128)} copy(f32[16,128,256]{2,1,0:T(8,128)} %copy-done.1) | data formatting | bytes 4194304 | tf_op jit(solution)/shard_map/div | solution.py:63
  37.3 1.8 gather_fusion.2
  40.8 12.9 %all_gather.9 = f32[16,512]{0,1:T(8,128)S(1)} all-gather(f32[16,128]{0,1:T(8,128)S(1)} %copy.325), channel_id=1, replica_groups=mesh['row'=8,'col'=4] {'col'}, dimensions={1}, use_global_device_ids=true | all-gather | bytes 40960 | tf_op jit(solution)/shard_map/all_gather | solution.py:80
  55.5 3.9 all-to-all-start
  62.6 1.8 pad_maximum_fusion
  65.7 2.5 copy.320
  70.7 5.1 collective-permute-start.3
  75.8 1.6 fusion.17
  79.9 2.1 copy.323
  82.1 8.4 %fusion.9 = f32[16,128,256]{2,1,0:T(8,128)} fusion(f32[16,130,1]{2,1,0:T(8,128)} %copy.323, f32[16,1,256]{2,1,0:T(1,128)} %copy-done.13, f32[16,128,256]{2,1,0:T(8,128)} %copy-done.1, f32[16,1,256]{2,1,0:T(1,128)} %copy-done.14, f32[16,130,1]{2,1,0:T(8,128)S(1)} %copy.321, f32[128,256]{1,0:T(8,128)S(1)} %broadcast_add_fusion), kind=kLoop, calls=%fused_computation.41 | loop fusion | flops 6815744 | bytes 4374784 | tf_op jit(solution)/shard_map/sub | solution.py:79
  90.5 9.9 %copy.326 = f32[16,128,256]{0,2,1:T(8,128)} copy(f32[16,128,256]{2,1,0:T(8,128)} %fusion.9) | data formatting | bytes 4194304 | tf_op jit(solution)/shard_map/sub | solution.py:79
  100.4 13.5 %scatter_fusion.1 = f32[16,128,256]{0,2,1:T(8,128)} fusion(f32[16,128,256]{0,2,1:T(8,128)} %copy.326, s32[128]{0:T(128)S(1)} %get-tuple-element.38, f32[128,16]{1,0:T(8,128)} %fusion.17), kind=kCustom, calls=%fused_computation.9 | custom fusion | flops 2048 | bytes 25600 | tf_op jit(solution)/shard_map/scatter-add | solution.py:98
  113.9 11.0 %copy.327 = f32[16,128,256]{2,1,0:T(8,128)} copy(f32[16,128,256]{0,2,1:T(8,128)} %scatter_fusion.1) | data formatting | bytes 4194304 | tf_op jit(solution)/shard_map/scatter-add | solution.py:98
  126.5 2.7 multiply_reduce_fusion.4
  129.2 28.6 %reduce-scatter.7.cloned.1.call-done = f32[16,128]{1,0:T(8,128)} async-done(((f32[16,1024]{1,0:T(8,128)}), f32[16,128]{1,0:T(8,128)}) %reduce-scatter.7.cloned.1.call-update) | async-done | bytes 8208 | tf_op jit(solution)/shard_map/reduce_scatter | solution.py:84
  158.7 38.0 %all-reduce = (f32[16]{0:T(128)S(1)}, f32[16]{0:T(128)S(1)}) all-reduce(f32[16]{0:T(128)S(1)} %add.278, f32[16]{0:T(128)S(1)} %add.287), channel_id=1, replica_groups=mesh['row'=8,'col'=4] {'row','col'}, use_global_device_ids=true, to_apply=%region_3.4 | all-reduce | flops 32 | bytes 256 | tf_op jit(solution)/shard_map/psum | solution.py:70
  196.8 4.0 multiply_reduce_fusion.3
  201.4 41.3 %psum.44 = f32[16]{0:T(128)S(1)} all-reduce(f32[16]{0:T(128)S(1)} %add.288), channel_id=1, replica_groups=mesh['row'=8,'col'=4] {'row','col'}, use_global_device_ids=true, to_apply=%region_12.14 | all-reduce | flops 16 | bytes 128 | tf_op jit(solution)/shard_map/psum | solution.py:70
  243.5 9.0 %all_gather.10 = f32[16,512]{1,0:T(8,128)S(1)} all-gather(f32[16,128]{1,0:T(8,128)S(1)} %multiply_add_fusion.6), channel_id=1, replica_groups=mesh['row'=8,'col'=4] {'col'}, dimensions={1}, use_global_device_ids=true | all-gather | bytes 40960 | tf_op jit(solution)/shard_map/all_gather | solution.py:80
  253.7 4.0 multiply_add_fusion.2
  257.7 9.9 %copy.338 = f32[16,128,256]{0,2,1:T(8,128)} copy(f32[16,128,256]{2,1,0:T(8,128)} %multiply_add_fusion.2) | data formatting | bytes 4194304 | tf_op jit(solution)/shard_map/add | solution.py:109
  269.3 3.9 all-to-all-start.1
  273.2 1.8 gather_fusion.3
  276.4 3.0 collective-permute-start.5
  280.6 1.4 gather_fusion.6
  283.2 1.8 pad_maximum_fusion.1
  286.3 2.4 copy.334
  291.3 7.2 %collective-permute-start.7 = (f32[16,130,1]{1,0,2:T(8,128)}, f32[16,130,1]{1,0,2:T(8,128)}, u32[]{:S(2)}, u32[]{:S(2)}) collective-permute-start(f32[16,130,1]{1,0,2:T(8,128)} %copy.336), channel_id=1, source_target_pairs={{0,1},{1,2},{2,3},{4,5},{5,6},{6,7},{8,9},{9,10},{10,11},{12,13},{... | collective-permute-start | bytes 24968 | tf_op jit(solution)/shard_map/ppermute | solution.py:16
  298.4 1.6 fusion.15
  301.2 2.1 copy.337
  303.4 8.3 %fusion.5 = f32[16,128,256]{2,1,0:T(8,128)} fusion(f32[16,130,1]{2,1,0:T(8,128)} %copy.337, f32[16,1,256]{2,1,0:T(1,128)} %copy-done.19, f32[16,128,256]{2,1,0:T(8,128)} %multiply_add_fusion.2, f32[16,1,256]{2,1,0:T(1,128)} %copy-done.20, f32[16,130,1]{2,1,0:T(8,128)S(1)} %copy.335, f32[128,256]{1,0:T(8,128)S(1)} %broadcast_add_fusion), kind=kLoop, calls=%fused_computation.29 | loop fusion | flops 6815744 | bytes 4374784 | tf_op jit(solution)/shard_map/sub | solution.py:79
  311.6 9.9 %copy.340 = f32[16,128,256]{0,2,1:T(8,128)} copy(f32[16,128,256]{2,1,0:T(8,128)} %fusion.5) | data formatting | bytes 4194304 | tf_op jit(solution)/shard_map/sub | solution.py:79
  321.5 13.5 %scatter_fusion.2 = f32[16,128,256]{0,2,1:T(8,128)} fusion(f32[16,128,256]{0,2,1:T(8,128)} %copy.340, s32[128]{0:T(128)S(1)} %get-tuple-element.38, f32[128,16]{1,0:T(8,128)} %fusion.15), kind=kCustom, calls=%fused_computation.10 | custom fusion | flops 2048 | bytes 25600 | tf_op jit(solution)/shard_map/scatter-add | solution.py:98
  335.1 11.0 %copy.341 = f32[16,128,256]{2,1,0:T(8,128)} copy(f32[16,128,256]{0,2,1:T(8,128)} %scatter_fusion.2) | data formatting | bytes 4194304 | tf_op jit(solution)/shard_map/scatter-add | solution.py:98
  347.7 2.5 multiply_reduce_fusion.2
  350.2 27.8 %reduce-scatter.11.cloned.1.call-done = f32[16,128]{1,0:T(8,128)} async-done(((f32[16,1024]{1,0:T(8,128)}), f32[16,128]{1,0:T(8,128)}) %reduce-scatter.11.cloned.1.call-update) | async-done | bytes 8208 | tf_op jit(solution)/shard_map/reduce_scatter | solution.py:84
  378.9 38.1 %psum.45 = f32[16]{0:T(128)S(1)} all-reduce(f32[16]{0:T(128)S(1)} %add.295), channel_id=1, replica_groups=mesh['row'=8,'col'=4] {'row','col'}, use_global_device_ids=true, to_apply=%region_18.20 | all-reduce | flops 16 | bytes 128 | tf_op jit(solution)/shard_map/psum | solution.py:100
  417.0 2.8 multiply_reduce_fusion.1
  420.4 41.3 %psum.46 = f32[16]{0:T(128)S(1)} all-reduce(f32[16]{0:T(128)S(1)} %add.297), channel_id=1, replica_groups=mesh['row'=8,'col'=4] {'row','col'}, use_global_device_ids=true, to_apply=%region_21.23 | all-reduce | flops 16 | bytes 128 | tf_op jit(solution)/shard_map/psum | solution.py:70
  461.8 5.0 multiply_add_fusion.1
  466.7 9.0 %all_gather.11 = f32[16,512]{1,0:T(8,128)S(1)} all-gather(f32[16,128]{1,0:T(8,128)S(1)} %multiply_add_fusion.4), channel_id=1, replica_groups=mesh['row'=8,'col'=4] {'col'}, dimensions={1}, use_global_device_ids=true | all-gather | bytes 40960 | tf_op jit(solution)/shard_map/all_gather | solution.py:80
  477.0 9.9 %copy.352 = f32[16,128,256]{0,2,1:T(8,128)} copy(f32[16,128,256]{2,1,0:T(8,128)} %multiply_add_fusion.1) | data formatting | bytes 4194304 | tf_op jit(solution)/shard_map/add | solution.py:109
  488.6 3.9 all-to-all-start.2
  492.5 1.8 gather_fusion.4
  495.7 3.0 collective-permute-start.9
  499.9 1.4 gather_fusion.7
  502.4 1.8 pad_maximum_fusion.2
  505.6 2.5 copy.348
  510.5 7.2 %collective-permute-start.11 = (f32[16,130,1]{1,0,2:T(8,128)}, f32[16,130,1]{1,0,2:T(8,128)}, u32[]{:S(2)}, u32[]{:S(2)}) collective-permute-start(f32[16,130,1]{1,0,2:T(8,128)} %copy.350), channel_id=1, source_target_pairs={{0,1},{1,2},{2,3},{4,5},{5,6},{6,7},{8,9},{9,10},{10,11},{12,13},{... | collective-permute-start | bytes 24968 | tf_op jit(solution)/shard_map/ppermute | solution.py:16
  517.7 1.6 fusion.13
  520.5 2.1 copy.351
  522.6 8.4 %fusion.1 = f32[16,128,256]{2,1,0:T(8,128)} fusion(f32[16,130,1]{2,1,0:T(8,128)} %copy.351, f32[16,1,256]{2,1,0:T(1,128)S(1)} %copy-done.16, f32[16,128,256]{2,1,0:T(8,128)} %multiply_add_fusion.1, f32[16,1,256]{2,1,0:T(1,128)S(1)} %copy-done.18, f32[16,130,1]{2,1,0:T(8,128)S(1)} %copy.349, f32[128,256]{1,0:T(8,128)S(1)} %broadcast_add_fusion), kind=kLoop, calls=%fused_computation.17 | loop fusion | flops 6815744 | bytes 4374784 | tf_op jit(solution)/shard_map/sub | solution.py:79
  531.0 9.9 %copy.354 = f32[16,128,256]{0,2,1:T(8,128)} copy(f32[16,128,256]{2,1,0:T(8,128)} %fusion.1) | data formatting | bytes 4194304 | tf_op jit(solution)/shard_map/sub | solution.py:79
  540.9 13.5 %scatter_fusion.3 = f32[16,128,256]{0,2,1:T(8,128)} fusion(f32[16,128,256]{0,2,1:T(8,128)} %copy.354, s32[128]{0:T(128)S(1)} %get-tuple-element.38, f32[128,16]{1,0:T(8,128)} %fusion.13), kind=kCustom, calls=%fused_computation.11 | custom fusion | flops 2048 | bytes 25600 | tf_op jit(solution)/shard_map/scatter-add | solution.py:98
  554.4 11.0 %copy.355 = f32[16,128,256]{2,1,0:T(8,128)} copy(f32[16,128,256]{0,2,1:T(8,128)} %scatter_fusion.3) | data formatting | bytes 4194304 | tf_op jit(solution)/shard_map/scatter-add | solution.py:98
  567.0 2.5 multiply_reduce_fusion
  569.6 27.8 %reduce-scatter.15.cloned.1.call-done = f32[16,128]{1,0:T(8,128)} async-done(((f32[16,1024]{1,0:T(8,128)}), f32[16,128]{1,0:T(8,128)}) %reduce-scatter.15.cloned.1.call-update) | async-done | bytes 8208 | tf_op jit(solution)/shard_map/reduce_scatter | solution.py:84
  598.2 37.9 %psum.47 = f32[16]{0:T(128)S(1)} all-reduce(f32[16]{0:T(128)S(1)} %add.304), channel_id=1, replica_groups=mesh['row'=8,'col'=4] {'row','col'}, use_global_device_ids=true, to_apply=%region_27.29 | all-reduce | flops 16 | bytes 128 | tf_op jit(solution)/shard_map/psum | solution.py:100
  636.8 5.0 multiply_add_fusion
  (216 shorter events, 50.6 us)
Async XLA Ops:
  7.2 46.5 %copy-start = (f32[512,1024]{1,0:T(8,128)S(1)}, f32[512,1024]{1,0:T(8,128)}, u32[]{:S(2)}) copy-start(f32[512,1024]{1,0:T(8,128)} %param.12) | copy-start | bytes 6291460
  7.2 122.1 %reduce-scatter.9.cloned.1.call-start = ((), (), s32[]{:S(2)}) async-start(), calls=%async_computation.10 | async-start | bytes 40960 | tf_op jit(solution)/shard_map/reduce_scatter | solution.py:95
  12.4 9.1 %copy-start.33 = (f32[128]{0:T(128)}, f32[128]{0:T(128)S(1)}, u32[]{:S(2)}) copy-start(f32[128]{0:T(128)S(1)} %broadcast_select_fusion) | copy-start | bytes 1540
  21.4 1.3 copy-start.1
  22.8 38.6 %collective-permute-start = (f32[16,1,256]{2,1,0:T(1,128)S(1)}, f32[16,1,256]{2,1,0:T(1,128)S(1)}, u32[]{:S(2)}, u32[]{:S(2)}) collective-permute-start(f32[16,1,256]{2,1,0:T(1,128)S(1)} %get-tuple-element.34), channel_id=1, source_target_pairs={{4,0},{8,4},{12,8},{16,12},{20,16},{24,20},{28,24},{5,1},{9,5},{13... | collective-permute-start | bytes 49160 | tf_op jit(solution)/shard_map/ppermute | solution.py:19
  24.1 16.2 %copy-start.11 = (f32[16,128]{1,0:T(8,128)S(1)}, f32[16,128]{1,0:T(8,128)}, u32[]{:S(2)}) copy-start(f32[16,128]{1,0:T(8,128)} %param.11) | copy-start | bytes 24580
  24.1 16.3 %copy-start.2 = (f32[4,32,32]{2,1,0:T(8,128)S(1)}, f32[4,32,32]{2,1,0:T(8,128)}, u32[]{:S(2)}) copy-start(f32[4,32,32]{2,1,0:T(8,128)} %param.13) | copy-start | bytes 49156
  24.1 37.3 %collective-permute-start.1 = (f32[16,1,256]{2,1,0:T(1,128)S(1)}, f32[16,1,256]{2,1,0:T(1,128)S(1)}, u32[]{:S(2)}, u32[]{:S(2)}) collective-permute-start(f32[16,1,256]{2,1,0:T(1,128)S(1)} %get-tuple-element.33), channel_id=1, source_target_pairs={{0,4},{4,8},{8,12},{12,16},{16,20},{20,24},{24,28},{1,5},{5,9},{9,... | collective-permute-start | bytes 49160 | tf_op jit(solution)/shard_map/ppermute | solution.py:16
  39.0 1.6 copy-start.3
  39.2 1.5 copy-start.21
  40.7 160.1 %copy-start.5 = (f32[16,128]{1,0:T(8,128)}, f32[16,128]{1,0:T(8,128)S(1)}, u32[]{:S(2)}) copy-start(f32[16,128]{1,0:T(8,128)S(1)} %reshape.280) | copy-start | bytes 24580
  55.5 69.4 %all-to-all-start = ((f32[16,4,2,128]{3,2,0,1:T(2,128)}), f32[16,4,2,128]{3,2,0,1:T(2,128)}, u32[]{:S(2)}, u32[]{:S(2)}) async-start(f32[16,4,2,128]{3,2,0,1:T(2,128)} %bitcast.100), calls=%async_computation | async-start | bytes 131072 | tf_op jit(solution)/shard_map/all_to_all | solution.py:83
  59.4 98.4 %reduce-scatter.7.cloned.1.call-start = ((), (), s32[]{:S(2)}) async-start(), calls=%async_computation.9 | async-start | bytes 73728 | tf_op jit(solution)/shard_map/reduce_scatter | solution.py:84
  60.2 1.2 copy-start.37
  61.4 0.6 copy-start.13
  62.0 0.6 copy-start.14
  68.2 10.6 %collective-permute-start.2 = (f32[16,130,1]{1,0,2:T(8,128)}, f32[16,130,1]{1,0,2:T(8,128)}, u32[]{:S(2)}, u32[]{:S(2)}) collective-permute-start(f32[16,130,1]{1,0,2:T(8,128)} %copy.320), channel_id=1, source_target_pairs={{1,0},{2,1},{3,2},{5,4},{6,5},{7,6},{9,8},{10,9},{11,10},{13,12},{... | collective-permute-start | bytes 24968 | tf_op jit(solution)/shard_map/ppermute | solution.py:19
  70.7 9.2 %collective-permute-start.3 = (f32[16,130,1]{1,0,2:T(8,128)}, f32[16,130,1]{1,0,2:T(8,128)}, u32[]{:S(2)}, u32[]{:S(2)}) collective-permute-start(f32[16,130,1]{1,0,2:T(8,128)} %copy.322), channel_id=1, source_target_pairs={{0,1},{1,2},{2,3},{4,5},{5,6},{6,7},{8,9},{9,10},{10,11},{12,13},{... | collective-permute-start | bytes 24968 | tf_op jit(solution)/shard_map/ppermute | solution.py:16
  126.5 31.4 %copy-start.12 = (f32[16,128]{1,0:T(8,128)S(1)}, f32[16,128]{1,0:T(8,128)}, u32[]{:S(2)}) copy-start(f32[16,128]{1,0:T(8,128)} %param.11) | copy-start | bytes 24580
  126.5 31.4 %copy-start.30 = (f32[128]{0:T(128)S(1)}, f32[128]{0:T(128)}, u32[]{:S(2)}) copy-start(f32[128]{0:T(128)} %dynamic_slice.3) | copy-start | bytes 1540
  196.8 4.0 copy-start.35
  196.8 4.0 copy-start.26
  196.8 4.0 copy-start.27
  200.9 51.6 %copy-start.9 = (f32[16,128]{1,0:T(8,128)}, f32[16,128]{1,0:T(8,128)S(1)}, u32[]{:S(2)}) copy-start(f32[16,128]{1,0:T(8,128)S(1)} %multiply_subtract_fusion.3) | copy-start | bytes 24580
  242.7 9.8 %copy-start.38 = (f32[16]{0:T(128)}, f32[16]{0:T(128)S(1)}, u32[]{:S(2)}) copy-start(f32[16]{0:T(128)S(1)} %psum.44) | copy-start | bytes 196
  257.7 21.8 %copy-start.22 = (f32[8,16]{1,0:T(8,128)S(1)}, f32[8,16]{1,0:T(8,128)}, u32[]{:S(2)}) copy-start(f32[8,16]{1,0:T(8,128)} %copy-done.21) | copy-start | bytes 1540
  269.3 76.8 %all-to-all-start.1 = ((f32[16,4,2,128]{3,2,0,1:T(2,128)}), f32[16,4,2,128]{3,2,0,1:T(2,128)}, u32[]{:S(2)}, u32[]{:S(2)}) async-start(f32[16,4,2,128]{3,2,0,1:T(2,128)} %bitcast.99), calls=%async_computation.3 | async-start | bytes 131072 | tf_op jit(solution)/shard_map/all_to_all | solution.py:83
  273.2 77.0 %reduce-scatter.13.cloned.1.call-start = ((), (), s32[]{:S(2)}) async-start(), calls=%async_computation.12 | async-start | bytes 40960 | tf_op jit(solution)/shard_map/reduce_scatter | solution.py:95
  275.0 7.0 %copy-start.4 = (f32[128,16]{1,0:T(8,128)}, f32[128,16]{1,0:T(8,128)S(1)}, u32[]{:S(2)}) copy-start(f32[128,16]{1,0:T(8,128)S(1)} %gather_fusion.3) | copy-start | bytes 24580
  275.1 6.9 %collective-permute-start.4 = (f32[16,1,256]{2,1,0:T(1,128)S(1)}, f32[16,1,256]{2,1,0:T(1,128)S(1)}, u32[]{:S(2)}, u32[]{:S(2)}) collective-permute-start(f32[16,1,256]{2,1,0:T(1,128)S(1)} %get-tuple-element.32), channel_id=1, source_target_pairs={{4,0},{8,4},{12,8},{16,12},{20,16},{24,20},{28,24},{5,1},{9,5},{13... | collective-permute-start | bytes 49160 | tf_op jit(solution)/shard_map/ppermute | solution.py:19
  276.4 5.6 collective-permute-start.5
  280.6 97.5 %reduce-scatter.11.cloned.1.call-start = ((), (), s32[]{:S(2)}) async-start(), calls=%async_computation.11 | async-start | bytes 73728 | tf_op jit(solution)/shard_map/reduce_scatter | solution.py:84
  282.0 0.6 copy-start.19
  282.6 0.6 copy-start.20
  288.8 11.3 %collective-permute-start.6 = (f32[16,130,1]{1,0,2:T(8,128)}, f32[16,130,1]{1,0,2:T(8,128)}, u32[]{:S(2)}, u32[]{:S(2)}) collective-permute-start(f32[16,130,1]{1,0,2:T(8,128)} %copy.334), channel_id=1, source_target_pairs={{1,0},{2,1},{3,2},{5,4},{6,5},{7,6},{9,8},{10,9},{11,10},{13,12},{... | collective-permute-start | bytes 24968 | tf_op jit(solution)/shard_map/ppermute | solution.py:19
  291.3 10.0 %collective-permute-start.7 = (f32[16,130,1]{1,0,2:T(8,128)}, f32[16,130,1]{1,0,2:T(8,128)}, u32[]{:S(2)}, u32[]{:S(2)}) collective-permute-start(f32[16,130,1]{1,0,2:T(8,128)} %copy.336), channel_id=1, source_target_pairs={{0,1},{1,2},{2,3},{4,5},{5,6},{6,7},{8,9},{9,10},{10,11},{12,13},{... | collective-permute-start | bytes 24968 | tf_op jit(solution)/shard_map/ppermute | solution.py:16
  347.6 30.4 %copy-start.31 = (f32[128]{0:T(128)S(1)}, f32[128]{0:T(128)}, u32[]{:S(2)}) copy-start(f32[128]{0:T(128)} %dynamic_slice.3) | copy-start | bytes 1540
  347.7 69.3 %copy-start.39 = (f32[16]{0:T(128)S(1)}, f32[16]{0:T(128)}, u32[]{:S(2)}) copy-start(f32[16]{0:T(128)} %copy-done.38) | copy-start | bytes 196
  417.0 44.8 %copy-start.28 = (f32[16]{0:T(128)}, f32[16]{0:T(128)S(1)}, u32[]{:S(2)}) copy-start(f32[16]{0:T(128)S(1)} %div.80) | copy-start | bytes 196
  417.0 2.8 copy-start.10
  417.0 2.8 copy-start.24
  417.0 2.8 copy-start.25
  461.7 5.1 copy-start.40
  461.8 5.0 copy-start.7
  476.9 21.8 %copy-start.23 = (f32[8,16]{1,0:T(8,128)S(1)}, f32[8,16]{1,0:T(8,128)}, u32[]{:S(2)}) copy-start(f32[8,16]{1,0:T(8,128)} %copy-done.21) | copy-start | bytes 1540
  488.6 76.8 %all-to-all-start.2 = ((f32[16,4,2,128]{3,2,0,1:T(2,128)}), f32[16,4,2,128]{3,2,0,1:T(2,128)}, u32[]{:S(2)}, u32[]{:S(2)}) async-start(f32[16,4,2,128]{3,2,0,1:T(2,128)} %bitcast.98), calls=%async_computation.6 | async-start | bytes 131072 | tf_op jit(solution)/shard_map/all_to_all | solution.py:83
  492.5 77.1 %reduce-scatter.17.cloned.1.call-start = ((), (), s32[]{:S(2)}) async-start(), calls=%async_computation.14 | async-start | bytes 40960 | tf_op jit(solution)/shard_map/reduce_scatter | solution.py:95
  494.4 6.9 %collective-permute-start.8 = (f32[16,1,256]{2,1,0:T(1,128)S(1)}, f32[16,1,256]{2,1,0:T(1,128)S(1)}, u32[]{:S(2)}, u32[]{:S(2)}) collective-permute-start(f32[16,1,256]{2,1,0:T(1,128)S(1)} %get-tuple-element.30), channel_id=1, source_target_pairs={{4,0},{8,4},{12,8},{16,12},{20,16},{24,20},{28,24},{5,1},{9,5},{13... | collective-permute-start | bytes 49160 | tf_op jit(solution)/shard_map/ppermute | solution.py:19
  495.7 5.6 collective-permute-start.9
  499.8 97.6 %reduce-scatter.15.cloned.1.call-start = ((), (), s32[]{:S(2)}) async-start(), calls=%async_computation.13 | async-start | bytes 73728 | tf_op jit(solution)/shard_map/reduce_scatter | solution.py:84
  501.2 0.6 copy-start.15
  501.8 0.6 copy-start.17
  505.5 12.1 %copy-start.34 = (f32[128]{0:T(128)S(1)}, f32[128]{0:T(128)}, u32[]{:S(2)}) copy-start(f32[128]{0:T(128)} %copy-done.33) | copy-start | bytes 1540
  508.0 11.3 %collective-permute-start.10 = (f32[16,130,1]{1,0,2:T(8,128)}, f32[16,130,1]{1,0,2:T(8,128)}, u32[]{:S(2)}, u32[]{:S(2)}) collective-permute-start(f32[16,130,1]{1,0,2:T(8,128)} %copy.348), channel_id=1, source_target_pairs={{1,0},{2,1},{3,2},{5,4},{6,5},{7,6},{9,8},{10,9},{11,10},{13,12},{... | collective-permute-start | bytes 24968 | tf_op jit(solution)/shard_map/ppermute | solution.py:19
  510.5 10.0 %collective-permute-start.11 = (f32[16,130,1]{1,0,2:T(8,128)}, f32[16,130,1]{1,0,2:T(8,128)}, u32[]{:S(2)}, u32[]{:S(2)}) collective-permute-start(f32[16,130,1]{1,0,2:T(8,128)} %copy.350), channel_id=1, source_target_pairs={{0,1},{1,2},{2,3},{4,5},{5,6},{6,7},{8,9},{9,10},{10,11},{12,13},{... | collective-permute-start | bytes 24968 | tf_op jit(solution)/shard_map/ppermute | solution.py:16
  519.3 3.3 copy-start.16
  519.3 3.3 copy-start.18
  567.0 30.4 %copy-start.8 = (f32[16,128]{1,0:T(8,128)S(1)}, f32[16,128]{1,0:T(8,128)}, u32[]{:S(2)}) copy-start(f32[16,128]{1,0:T(8,128)} %copy-done.7) | copy-start | bytes 24580
  567.0 30.4 %copy-start.32 = (f32[128]{0:T(128)S(1)}, f32[128]{0:T(128)}, u32[]{:S(2)}) copy-start(f32[128]{0:T(128)} %dynamic_slice.3) | copy-start | bytes 1540
  567.0 69.1 %copy-start.41 = (f32[16]{0:T(128)S(1)}, f32[16]{0:T(128)}, u32[]{:S(2)}) copy-start(f32[16]{0:T(128)} %copy-done.40) | copy-start | bytes 196
  567.0 69.1 %copy-start.6 = (f32[16,128]{1,0:T(8,128)S(1)}, f32[16,128]{1,0:T(8,128)}, u32[]{:S(2)}) copy-start(f32[16,128]{1,0:T(8,128)} %copy-done.5) | copy-start | bytes 24580
  567.0 69.1 %copy-start.29 = (f32[16]{0:T(128)S(1)}, f32[16]{0:T(128)}, u32[]{:S(2)}) copy-start(f32[16]{0:T(128)} %copy-done.28) | copy-start | bytes 196
  567.0 69.1 %copy-start.36 = (f32[16]{0:T(128)S(1)}, f32[16]{0:T(128)}, u32[]{:S(2)}) copy-start(f32[16]{0:T(128)} %copy-done.35) | copy-start | bytes 196
Sparse Core Ops, SparseCore 0:
  40.4 27.7 reduce-scatter.8
  126.6 31.2 reduce-scatter.6
  280.7 24.5 reduce-scatter.12
  347.8 30.2 reduce-scatter.10
  499.9 24.5 reduce-scatter.16
  567.1 30.2 reduce-scatter.14
where the time goes:
time: 654 us; the launch traced here: 649 us
  blocking collectives  227 us (35%)
  local copies, waits for them, and re-layouts  150 us (23%)
  other arithmetic  120 us (18%)
  waiting for transfers between devices  84.5 us (13%)
  starting transfers between devices  48.3 us (7%)
  between operations  14.9 us (2%)
    psum x3, blocking collectives, norm_sum(): return lax.psum(inner(ad, ap, bd, bp), ('row', 'col'))  121 us
    reduce_scatter x3, waiting for transfers between devices, body(): lax.psum_scatter(moved.reshape(batch, nrows * local_n), 'row', scatter_di...  84.3 us
    psum x2, blocking collectives, body(): alpha = rz / lax.psum(inner(pd, pp, die, qp), ('row', 'col'))  76 us
    scatter-add x3, other arithmetic, body(): die = die.at[:, loc_r, loc_c].add(cond_sel * (at_bumps - pkg_at))  40.5 us
    scatter-add x3, local copies, waits for them, and re-layouts, body(): die = die.at[:, loc_r, loc_c].add(cond_sel * (at_bumps - pkg_at))  33 us
    all_gather x3, blocking collectives, body(): segment = lax.all_gather(pp, 'col', axis=1, tiled=True)  30.8 us
    sub x3, local copies, waits for them, and re-layouts, body(): die = (4.0 + die_shunt) * pd - beside_all  29.7 us
    ppermute x6, starting transfers between devices, with_halo(): lax.ppermute(lax.slice_in_dim(block, block.shape[dim] - width, None, axis...  28.7 us
  transfers between devices with their start and end apart: 21, of which 3 were waited for; matrix products, arithmetic and copies ran while one was open for 31% of the time, Pallas kernels for 0%

commit v1 on v0

v1 whole, which is shorter than its diff:
```python
import functools

import jax
import jax.numpy as jnp
from jax import lax
from jax.experimental import pallas as pl
from jax.experimental.pallas import tpu as pltpu
from jax.sharding import PartitionSpec as P

BUMP_C = 64
PB = 32
ITERS = 3
MESH = pl.DeviceIdType.MESH
HI = lax.Precision.HIGHEST
F32 = jnp.float32


def drain(ref, sem):
    pltpu.make_async_copy(ref, ref, sem).wait()


def kernel(
    nrows, ncols, lat_rows, lat_cols,
    rd_ref, shunt_ref, rp_ref, mat_ref, inv_ref, locr_ref, locc_ref, cexp_ref, chere_ref,
    xd_ref, xp_ref,
    us, ws, rbuf, diag, invd, mask, cmask, mh, ml, bd, gbuf, dbuf, cf, abuf, vpx,
    rsend, hr, csend, hc, seg, part, rec, cont, dat, red,
    hsend, hrecv, ssend, srecv, psend, precv, csendm, drecv, rsendm, rrecv, selfsem,
):
    ndev = nrows * ncols
    irow = lax.axis_index("row")
    icol = lax.axis_index("col")
    me = irow * ncols + icol
    batch, tile_r, tile_c = rd_ref.shape
    local_n = rp_ref.shape[1]
    cell_r = tile_r // lat_rows
    cell_c = tile_c // lat_cols

    hr[...] = jnp.zeros_like(hr)
    hc[...] = jnp.zeros_like(hc)
    barrier = pltpu.get_barrier_semaphore()

    def greet(d, c):
        t = lax.rem(me + d, ndev)
        pl.semaphore_signal(
            barrier, inc=1, device_id=(t // ncols, lax.rem(t, ncols)), device_id_type=MESH
        )
        return c

    lax.fori_loop(1, ndev, greet, 0)

    row_c = lax.broadcasted_iota(jnp.int32, (cell_r, tile_c), 0)
    lane_c = lax.rem(lax.broadcasted_iota(jnp.int32, (cell_r, tile_c), 1), cell_c)
    for lr in range(lat_rows):
        rs = slice(lr * cell_r, (lr + 1) * cell_r)
        hit = (row_c == locr_ref[lr : lr + 1, :]) & (lane_c == locc_ref[lr : lr + 1, :])
        m = jnp.where(hit, 1.0, 0.0)
        cm = m * cexp_ref[lr : lr + 1, :]
        mask[rs, :] = m
        cmask[rs, :] = cm
        dg = 4.0 + shunt_ref[rs, :] + cm
        diag[rs, :] = dg
        invd[rs, :] = 1.0 / dg
    bd[...] = jnp.zeros_like(bd)
    for q in range(local_n // PB):
        bd[q * PB : (q + 1) * PB, q * PB : (q + 1) * PB] = inv_ref[q]
    high = mat_ref[...].astype(jnp.bfloat16)
    mh[...] = high
    ml[...] = (mat_ref[...] - high.astype(F32)).astype(jnp.bfloat16)

    node_c = icol * lat_cols + lax.broadcasted_iota(jnp.int32, (tile_c, local_n), 0) // cell_c
    node_l = lax.broadcasted_iota(jnp.int32, (tile_c, local_n), 1)
    embeds = {}

    def embed(lr, j):
        off = lr * BUMP_C - j * local_n
        if off not in embeds:
            embeds[off] = jnp.where(node_c + off == node_l, 1.0, 0.0)
        return embeds[off]

    def meets(lr, j):
        return lr * BUMP_C < (j + 1) * local_n and j * local_n < (lr + 1) * BUMP_C

    lane_e = lax.broadcasted_iota(jnp.int32, (tile_r, 128), 1)
    row_i = lax.broadcasted_iota(jnp.int32, (tile_r, tile_c), 0)
    lane_i = lax.broadcasted_iota(jnp.int32, (tile_r, tile_c), 1)
    sub_k = lax.broadcasted_iota(jnp.int32, (batch, 128), 0)
    lane_k = lax.broadcasted_iota(jnp.int32, (batch, 128), 1)

    def remote(src, dst, ssem, rsem, r, c):
        return pltpu.make_async_remote_copy(
            src_ref=src, dst_ref=dst, send_sem=ssem, recv_sem=rsem,
            device_id=(r, c), device_id_type=MESH,
        )

    has = (irow > 0, irow < nrows - 1, icol > 0, icol < ncols - 1)

    def halos(it):
        return (
            remote(rsend.at[it, 0], hr.at[it, 1], hsend.at[it, 0], hrecv.at[it, 1], irow - 1, icol),
            remote(rsend.at[it, 1], hr.at[it, 0], hsend.at[it, 1], hrecv.at[it, 0], irow + 1, icol),
            remote(csend.at[it, 0], hc.at[it, 1], hsend.at[it, 2], hrecv.at[it, 3], irow, icol - 1),
            remote(csend.at[it, 1], hc.at[it, 0], hsend.at[it, 3], hrecv.at[it, 2], irow, icol + 1),
        )

    def put(slot, value):
        cf[slot] = jnp.broadcast_to(value, (batch, tile_c))

    rp = rp_ref[...]
    ups, gs, sp, alphas, betas = [], [], None, [], []
    chere = chere_ref[...]

    for it in range(ITERS):
        up = lax.dot_general(rp, bd[...], (((1,), (1,)), ((), ())), precision=HI)
        ups.append(up)
        seg[it, icol] = up
        if it == 0:
            pl.semaphore_wait(barrier, ndev - 1)
        for d in range(1, ncols):
            remote(
                seg.at[it, icol], seg.at[it, icol], ssend.at[it], srecv.at[it],
                irow, lax.rem(icol + d, ncols),
            ).start()

        def phase_u(k, e):
            one = pl.ds(k, 1)
            if it == 0:
                r = rd_ref[k]
            elif it == 1:
                r = rd_ref[k] - cf[0, one, :] * ws[0, k]
                rbuf[k] = r
            else:
                r = rbuf[k] - (cf[1, one, :] * ws[1, k] + cf[2, one, :] * ws[0, k])
            u = r * invd[...]
            us[it, k] = u
            gbuf[one, :] = jnp.sum(r * u, axis=0, keepdims=True)
            rsend[it, 0, one, :] = u[0:1, :]
            rsend[it, 1, one, :] = u[tile_r - 1 : tile_r, :]
            mu = u * mask[...]
            for lr in range(lat_rows):
                abuf[lr, one, :] = jnp.sum(
                    mu[lr * cell_r : (lr + 1) * cell_r], axis=0, keepdims=True
                )
            e = jnp.where(lane_e == k, u[:, 0:1], e)
            return jnp.where(lane_e == k + batch, u[:, tile_c - 1 : tile_c], e)

        e = lax.fori_loop(0, batch, phase_u, jnp.zeros((tile_r, 128), F32))
        et = e.T
        csend[it, 0] = et[0:batch, :]
        csend[it, 1] = et[batch : 2 * batch, :]
        for side, copy in enumerate(halos(it)):
            pl.when(has[side])(copy.start)
        for j in range(ncols):
            total = jnp.zeros((batch, local_n), F32)
            for lr in range(lat_rows):
                if meets(lr, j):
                    total += jnp.dot(abuf[lr], embed(lr, j), precision=HI)
            cont[it, j] = total
        dat[it, icol] = cont[it, icol]
        for d in range(1, ncols):
            t = lax.rem(icol + d, ncols)
            remote(
                cont.at[it, t], dat.at[it, icol], csendm.at[it], drecv.at[it], irow, t
            ).start()

        drain(seg.at[it, 0 : ncols - 1], srecv.at[it])
        acc = None
        for j in range(ncols):
            v = seg[it, j]
            vh = v.astype(jnp.bfloat16)
            vl = (v - vh.astype(F32)).astype(jnp.bfloat16)
            ks = slice(j * local_n, (j + 1) * local_n)
            both = jnp.dot(
                jnp.concatenate([vh, vl], axis=0), mh[ks, :], preferred_element_type=F32
            )
            term = both[:batch] + both[batch:]
            term += jnp.dot(vh, ml[ks, :], preferred_element_type=F32)
            acc = term if acc is None else acc + term
        for m in range(nrows):
            part[it, m] = acc[:, m * local_n : (m + 1) * local_n]
        for m in range(nrows):
            n = icol * nrows + m
            copy = remote(
                part.at[it, m], rec.at[it, irow], psend.at[it], precv.at[it],
                n // ncols, lax.rem(n, ncols),
            )
            pl.when(n != me)(copy.start)

            @pl.when(n == me)
            def _():
                pltpu.make_async_copy(part.at[it, m], rec.at[it, irow], precv.at[it]).start()

        for lr in range(lat_rows):
            total = jnp.zeros((batch, tile_c), F32)
            for j in range(ncols):
                if meets(lr, j):
                    total += lax.dot_general(
                        seg[it, j], embed(lr, j), (((1,), (1,)), ((), ())), precision=HI
                    )
            vpx[lr] = total

        for side, index in enumerate(((hr, 0), (hr, 1), (hc, 0), (hc, 1))):
            ref, pos = index

            @pl.when(has[side])
            def _():
                drain(ref.at[it, pos], hrecv.at[it, side])

        ct = jnp.concatenate(
            [hc[it, 0], hc[it, 1], jnp.zeros((128 - 2 * batch, tile_r), F32)], axis=0
        ).T

        def phase_w(k, c):
            one = pl.ds(k, 1)
            u = us[it, k]
            left = jnp.sum(jnp.where(lane_e == k, ct, 0.0), axis=1, keepdims=True)
            right = jnp.sum(jnp.where(lane_e == k + batch, ct, 0.0), axis=1, keepdims=True)
            near = jnp.where(row_i == 0, hr[it, 0, one, :], pltpu.roll(u, 1, 0))
            near += jnp.where(row_i == tile_r - 1, hr[it, 1, one, :], pltpu.roll(u, tile_r - 1, 0))
            near += jnp.where(lane_i == 0, left, pltpu.roll(u, 1, 1))
            near += jnp.where(lane_i == tile_c - 1, right, pltpu.roll(u, tile_c - 1, 1))
            feed = jnp.concatenate(
                [
                    cmask[lr * cell_r : (lr + 1) * cell_r, :] * vpx[lr, one, :]
                    for lr in range(lat_rows)
                ],
                axis=0,
            )
            w = diag[...] * u - near - feed
            if it + 1 < ITERS:
                ws[it, k] = w
            dbuf[one, :] = jnp.sum(w * u, axis=0, keepdims=True)
            return c

        lax.fori_loop(0, batch, phase_w, 0)

        drain(rec.at[it], precv.at[it])
        drain(dat.at[it, 0 : ncols - 1], drecv.at[it])
        qp = rec[it, 0]
        for i in range(1, nrows):
            qp += rec[it, i]
        die_at = dat[it, 0]
        for j in range(1, ncols):
            die_at += dat[it, j]
        qp += chere * (up - die_at)
        g = jnp.sum(gbuf[...], axis=1, keepdims=True) + jnp.sum(rp * up, axis=1, keepdims=True)
        d = jnp.sum(dbuf[...], axis=1, keepdims=True) + jnp.sum(up * qp, axis=1, keepdims=True)
        line = jnp.where(lane_k == sub_k, g, 0.0) + jnp.where(lane_k == sub_k + batch, d, 0.0)
        red[it, me] = jnp.sum(line, axis=0, keepdims=True)

        def spread(d, c):
            t = lax.rem(me + d, ndev)
            remote(
                red.at[it, me], red.at[it, me], rsendm.at[it], rrecv.at[it],
                t // ncols, lax.rem(t, ncols),
            ).start()
            return c

        lax.fori_loop(1, ndev, spread, 0)
        drain(red.at[it, 0 : ndev - 1], rrecv.at[it])
        line = jnp.sum(red[it], axis=0)
        g = jnp.sum(jnp.where(lane_k == sub_k, line, 0.0), axis=1, keepdims=True)
        d = jnp.sum(jnp.where(lane_k == sub_k + batch, line, 0.0), axis=1, keepdims=True)
        if it == 0:
            alpha = g / d
            sp = qp
            put(0, alpha)
        else:
            beta = g / gs[-1]
            betas.append(beta)
            alpha = g / (d - beta * g / alphas[-1])
            sp = qp + beta * sp
            if it == 1:
                put(1, alpha)
                put(2, alpha * beta)
        gs.append(g)
        alphas.append(alpha)
        rp = rp - alpha * sp

    c2 = alphas[2]
    c1 = alphas[1] + c2 * betas[1]
    c0 = alphas[0] + c1 * betas[0]
    put(0, c0)
    put(1, c1)
    put(2, c2)
    xp_ref[...] = c0 * ups[0] + c1 * ups[1] + c2 * ups[2]

    def finish(k, c):
        one = pl.ds(k, 1)
        xd_ref[k] = cf[0, one, :] * us[0, k] + cf[1, one, :] * us[1, k] + cf[2, one, :] * us[2, k]
        return c

    lax.fori_loop(0, batch, finish, 0)

    mine = me // nrows == icol
    for it in range(ITERS):
        drain(seg.at[it, 0 : ncols - 1], ssend.at[it])
        drain(cont.at[it, 0 : ncols - 1], csendm.at[it])
        drain(red.at[it, 0 : ndev - 1], rsendm.at[it])

        @pl.when(mine)
        def _():
            drain(part.at[it, 0 : nrows - 1], psend.at[it])

        @pl.when(jnp.logical_not(mine))
        def _():
            drain(part.at[it], psend.at[it])

        for side, copy in enumerate(halos(it)):
            pl.when(has[side])(copy.wait_send)


def solution(mesh):
    nrows, ncols = mesh.shape["row"], mesh.shape["col"]

    def body(die_current, die_shunt, pkg_current, pkg_matrix, pkg_block_inv, bump_node, bump_conductance):
        irow = lax.axis_index("row")
        icol = lax.axis_index("col")
        batch, tile_r, tile_c = die_current.shape
        local_n = pkg_current.shape[1]
        bumps = bump_node.shape[0]
        lat_rows = bumps // BUMP_C // nrows
        lat_cols = BUMP_C // ncols
        cell_r, cell_c = tile_r // lat_rows, tile_c // lat_cols
        total_c = tile_c * ncols
        at = (irow * lat_rows, icol * lat_cols)
        nodes = lax.dynamic_slice(bump_node.reshape(-1, BUMP_C), at, (lat_rows, lat_cols))
        cond = lax.dynamic_slice(bump_conductance.reshape(-1, BUMP_C), at, (lat_rows, lat_cols))
        nodes = jnp.repeat(nodes, cell_c, axis=1)
        cond = jnp.repeat(cond, cell_c, axis=1)
        loc_r = (nodes // total_c) % cell_r
        loc_c = (nodes % total_c) % cell_c
        here = lax.dynamic_slice_in_dim(
            bump_conductance, (irow * ncols + icol) * local_n, local_n
        ).reshape(1, local_n)
        ndev = nrows * ncols
        vm = pltpu.VMEM
        dma = pltpu.SemaphoreType.DMA
        row = (batch, tile_c)
        return pl.pallas_call(
            functools.partial(kernel, nrows, ncols, lat_rows, lat_cols),
            out_shape=(
                jax.ShapeDtypeStruct(die_current.shape, F32),
                jax.ShapeDtypeStruct(pkg_current.shape, F32),
            ),
            in_specs=[pl.BlockSpec(memory_space=pltpu.VMEM)] * 9,
            out_specs=(pl.BlockSpec(memory_space=pltpu.VMEM),) * 2,
            scratch_shapes=[
                vm((ITERS,) + die_current.shape, F32),
                vm((ITERS - 1,) + die_current.shape, F32),
                vm(die_current.shape, F32),
                vm((tile_r, tile_c), F32),
                vm((tile_r, tile_c), F32),
                vm((tile_r, tile_c), F32),
                vm((tile_r, tile_c), F32),
                vm(pkg_matrix.shape, jnp.bfloat16),
                vm(pkg_matrix.shape, jnp.bfloat16),
                vm((local_n, local_n), F32),
                vm(row, F32),
                vm(row, F32),
                vm((3,) + row, F32),
                vm((lat_rows,) + row, F32),
                vm((lat_rows,) + row, F32),
                vm((ITERS, 2) + row, F32),
                vm((ITERS, 2) + row, F32),
                vm((ITERS, 2, batch, tile_r), F32),
                vm((ITERS, 2, batch, tile_r), F32),
                vm((ITERS, ncols, batch, local_n), F32),
                vm((ITERS, nrows, batch, local_n), F32),
                vm((ITERS, nrows, batch, local_n), F32),
                vm((ITERS, ncols, batch, local_n), F32),
                vm((ITERS, ncols, batch, local_n), F32),
                vm((ITERS, ndev, 1, 128), F32),
                dma((ITERS, 4)),
                dma((ITERS, 4)),
                dma((ITERS,)),
                dma((ITERS,)),
                dma((ITERS,)),
                dma((ITERS,)),
                dma((ITERS,)),
                dma((ITERS,)),
                dma((ITERS,)),
                dma((ITERS,)),
                dma((ITERS,)),
            ],
            compiler_params=pltpu.CompilerParams(
                collective_id=0, has_side_effects=True, vmem_limit_bytes=48 << 20
            ),
        )(die_current, die_shunt, pkg_current, pkg_matrix, pkg_block_inv, loc_r, loc_c, cond, here)

    placed = (
        P(None, "row", "col"),
        P("row", "col"),
        P(None, ("row", "col")),
        P("row", "col"),
        P(("row", "col"), None, None),
        P(),
        P(),
    )
    return jax.shard_map(
        body,
        mesh=mesh,
        in_specs=placed,
        out_specs=(P(None, "row", "col"), P(None, ("row", "col"))),
        check_vma=False,
    )
```

time: 654 us -> 60.3 us (0.09)
  blocking collectives: 227 us -> 0 us
  local copies, waits for them, and re-layouts: 150 us -> 8.77 us
  other arithmetic: 120 us -> 0.02 us
  waiting for transfers between devices: 84.5 us -> 0 us
  Pallas kernels: 0 us -> 50.4 us
  starting transfers between devices: 48.3 us -> 0 us
  between operations: 14.9 us -> 0.68 us
    psum x5 -> x0, blocking collectives: 197 us -> none  [the longest x3 121 us: norm_sum(): return lax.psum(inner(ad, ap, bd, bp), ('row', 'col'))]
    reduce_scatter x6 -> x0, waiting for transfers between devices: 84.3 us -> none  [the longest x3 84.3 us: body(): lax.psum_scatter(moved.reshape(batch, nrows * local_n), 'row', scatter_di...]
    pallas_call x0 -> x1, Pallas kernels: none -> 50.4 us  [body(): pl.pallas_call(functools.partial(kernel, nrows, ncols, lat_rows, lat_cols...]
    scatter-add x4 -> x0, other arithmetic: 47.8 us -> none  [the longest x3 40.5 us: body(): die = die.at[:, loc_r, loc_c].add(cond_sel * (at_bumps - pkg_at))]
    ppermute x12 -> x0, starting transfers between devices: 36.4 us -> none  [the longest x6 28.7 us: with_halo(): lax.ppermute(lax.slice_in_dim(block, block.shape[dim] - width, None, axis...]
    scatter-add x3 -> x0, local copies, waits for them, and re-layouts: 33 us -> none  [body(): die = die.at[:, loc_r, loc_c].add(cond_sel * (at_bumps - pkg_at))]
    all_gather x3 -> x0, blocking collectives: 30.8 us -> none  [body(): segment = lax.all_gather(pp, 'col', axis=1, tiled=True)]
    sub x3 -> x0, local copies, waits for them, and re-layouts: 29.7 us -> none  [body(): die = (4.0 + die_shunt) * pd - beside_all]
  transfers between devices with their start and end apart: 21 -> 0, of which waited for: 3 -> 0; matrix products, arithmetic and copies ran while one was open for 31% -> 0% of each run, Pallas kernels for 0% -> 0%
where the time goes in v1:
time: 60.3 us; the launch traced here: 59.9 us
  Pallas kernels  50.4 us (84%)
  local copies, waits for them, and re-layouts  8.77 us (15%)
  between operations  0.68 us (1%)
    pallas_call x1, Pallas kernels, body(): pl.pallas_call(functools.partial(kernel, nrows, ncols, lat_rows, lat_cols...  50.4 us
    unnamed x10, local copies, waits for them, and re-layouts  5.94 us

profile of v1, /device:TPU:0, one launch (start us, length us, event | category | flops | bytes accessed | tf_op | source)
XLA Modules:
  0.0 59.9 jit_solution(11270400349930159829)
XLA Ops:
  0.6 0.8 %dynamic-slice_bitcast_fusion.chere_ref = f32[1,128]{1,0:T(1,128)S(1)} fusion(f32[4096]{0:T(1024)} %param.13, s32[]{:T(128)S(6)} %select_n.37), kind=kLoop, calls=%fused_computation.16 | loop fusion | bytes 1028 | tf_op jit(solution)/shard_map/reshape | solution.py:335
  1.4 0.8 %reshape.19 = s32[64,64]{1,0:T(8,128)S(1)} reshape(s32[4096]{0:T(1024)} %param.12) | data formatting | bytes 32768 | tf_op jit(solution)/shard_map/reshape | solution.py:327
  2.2 0.1 dynamic_slice.9
  2.3 0.8 %reshape.21 = f32[64,64]{1,0:T(8,128)S(1)} reshape(f32[4096]{0:T(1024)} %param.13) | data formatting | bytes 32768 | tf_op jit(solution)/shard_map/reshape | solution.py:328
  3.0 0.1 dynamic_slice.10
  3.1 0.1 broadcast_in_dim.7
  3.2 0.1 reshape.22.cexp_ref
  3.3 0.1 broadcast_in_dim.6
  3.4 0.1 reshape.20
  3.5 0.0 copy-start
  3.5 1.6 %copy-done = f32[16,128,256]{2,1,0:T(8,128)S(1)} copy-done((f32[16,128,256]{2,1,0:T(8,128)S(1)}, f32[16,128,256]{2,1,0:T(8,128)}, u32[]{:S(2)}) %copy-start) | copy-done | bytes 2097176
  5.1 0.0 copy-start.1
  5.1 0.9 %copy-done.1 = f32[128,256]{1,0:T(8,128)S(1)} copy-done((f32[128,256]{1,0:T(8,128)S(1)}, f32[128,256]{1,0:T(8,128)}, u32[]{:S(2)}) %copy-start.1) | copy-done | bytes 131096
  6.0 0.0 copy-start.2
  6.0 0.8 %copy-done.2 = f32[4,32,32]{2,1,0:T(8,128)S(1)} copy-done((f32[4,32,32]{2,1,0:T(8,128)S(1)}, f32[4,32,32]{2,1,0:T(8,128)}, u32[]{:S(2)}) %copy-start.2) | copy-done | bytes 16408
  6.8 0.0 copy-start.3
  6.8 0.7 %copy-done.3 = f32[16,128]{1,0:T(8,128)S(1)} copy-done((f32[16,128]{1,0:T(8,128)S(1)}, f32[16,128]{1,0:T(8,128)}, u32[]{:S(2)}) %copy-start.3) | copy-done | bytes 8216
  7.5 50.4 %shard_map.86 = (f32[16,128,256]{2,1,0:T(8,128)S(1)}, f32[16,128]{1,0:T(8,128)S(1)}) custom-call(f32[16,128,256]{2,1,0:T(8,128)S(1)} %copy-done, f32[128,256]{1,0:T(8,128)S(1)} %copy-done.1, f32[16,128]{1,0:T(8,128)S(1)} %copy-done.3, f32[512,1024]{1,0:T(8,128)} %mat_ref.1, f32[4,32,32]{2,1,0:T(8,128)S(1)} %copy-done.2, ...), custom_call_target="tpu_custom_call" | custom-call | tf_op jit(solution)/shard_map/pallas_call | solution.py:340
  57.9 1.3 %copy.11 = f32[16,128,256]{2,1,0:T(8,128)} copy(f32[16,128,256]{2,1,0:T(8,128)S(1)} %get-tuple-element.6) | data formatting | bytes 4194304
  59.3 0.6 copy.12
  (1 shorter events, 0.0 us)
Async XLA Ops:
  3.5 1.6 %copy-start = (f32[16,128,256]{2,1,0:T(8,128)S(1)}, f32[16,128,256]{2,1,0:T(8,128)}, u32[]{:S(2)}) copy-start(f32[16,128,256]{2,1,0:T(8,128)} %rd_ref.1) | copy-start | bytes 6291460
  5.1 0.9 %copy-start.1 = (f32[128,256]{1,0:T(8,128)S(1)}, f32[128,256]{1,0:T(8,128)}, u32[]{:S(2)}) copy-start(f32[128,256]{1,0:T(8,128)} %shunt_ref.1) | copy-start | bytes 393220
  6.0 0.8 %copy-start.2 = (f32[4,32,32]{2,1,0:T(8,128)S(1)}, f32[4,32,32]{2,1,0:T(8,128)}, u32[]{:S(2)}) copy-start(f32[4,32,32]{2,1,0:T(8,128)} %inv_ref.1) | copy-start | bytes 49156
  6.8 0.7 %copy-start.3 = (f32[16,128]{1,0:T(8,128)S(1)}, f32[16,128]{1,0:T(8,128)}, u32[]{:S(2)}) copy-start(f32[16,128]{1,0:T(8,128)} %rp_ref.1) | copy-start | bytes 24580

commit v2 on v1

v2 whole, which is shorter than its diff:
```python
import functools

import jax
import jax.numpy as jnp
from jax import lax
from jax.experimental import pallas as pl
from jax.experimental.pallas import tpu as pltpu
from jax.sharding import PartitionSpec as P

BUMP_C = 64
PB = 32
ITERS = 3
MESH = pl.DeviceIdType.MESH
HI = lax.Precision.HIGHEST
F32 = jnp.float32


def drain(ref, sem):
    pltpu.make_async_copy(ref, ref, sem).wait()


def split3(v):
    high = v.astype(jnp.bfloat16)
    rest = v - high.astype(F32)
    mid = rest.astype(jnp.bfloat16)
    return [high, mid, (rest - mid.astype(F32)).astype(jnp.bfloat16)]


def exact_pick(parts, onehot):
    rows = sum(p.shape[0] for p in parts)
    stacked = jnp.concatenate(parts, axis=0) if len(parts) > 1 else parts[0]
    out = jnp.dot(
        jnp.concatenate(split3(stacked), axis=0), onehot, preferred_element_type=F32
    )
    return out[:rows] + out[rows : 2 * rows] + out[2 * rows :]


def pairs_by_offset(lat_rows, ncols, local_n):
    groups = {}
    for lr in range(lat_rows):
        for j in range(ncols):
            if lr * BUMP_C < (j + 1) * local_n and j * local_n < (lr + 1) * BUMP_C:
                groups.setdefault(lr * BUMP_C - j * local_n, []).append((lr, j))
    return sorted(groups.items())


def kernel(
    nrows, ncols, lat_rows, lat_cols,
    rd_hbm, shunt_ref, rp_ref, mat_hbm, inv_ref, node_ref, cond_ref,
    xd_ref, xp_ref,
    rd_ref, mat_ref, us, ms, ks, diag, invd, mask, cinv, mh, ml, bd, gbuf, dbuf, cf, abuf, vpx,
    emb, embt, rsend, hr, csend, hc, seg, part, rec, cont, dat, red,
    hsend, hrecv, ssend, srecv, psend, precv, csendm, drecv, rsendm, rrecv, loadsem,
):
    ndev = nrows * ncols
    irow = lax.axis_index("row")
    icol = lax.axis_index("col")
    me = irow * ncols + icol
    batch, tile_r, tile_c = rd_ref.shape
    local_n = rp_ref.shape[1]
    cell_r = tile_r // lat_rows
    cell_c = tile_c // lat_cols
    total_c = tile_c * ncols
    groups = pairs_by_offset(lat_rows, ncols, local_n)

    load_rd = pltpu.make_async_copy(rd_hbm, rd_ref, loadsem.at[0])
    load_mat = pltpu.make_async_copy(mat_hbm, mat_ref, loadsem.at[1])
    load_rd.start()
    load_mat.start()

    hr[...] = jnp.zeros_like(hr)
    hc[...] = jnp.zeros_like(hc)
    barrier = pltpu.get_barrier_semaphore()

    def greet(d, c):
        t = lax.rem(me + d, ndev)
        pl.semaphore_signal(
            barrier, inc=1, device_id=(t // ncols, lax.rem(t, ncols)), device_id_type=MESH
        )
        return c

    lax.fori_loop(1, ndev, greet, 0)

    seg_rows = lat_rows * BUMP_C // 128
    per_row = 128 // BUMP_C
    nodes = node_ref[pl.ds(irow * seg_rows, seg_rows), :]
    conds = cond_ref[pl.ds(irow * seg_rows, seg_rows), :]
    node_r = lax.rem(nodes // total_c, cell_r).astype(F32)
    node_q = lax.rem(lax.rem(nodes, total_c), cell_c).astype(F32)
    tall = jnp.concatenate([node_r, node_q, conds], axis=0)
    tall = jnp.concatenate([tall, jnp.zeros((-tall.shape[0] % 8, 128), F32)], axis=0)
    wide_l = lax.broadcasted_iota(jnp.int32, (128, tile_c), 0)
    wide_c = lax.broadcasted_iota(jnp.int32, (128, tile_c), 1) // cell_c + icol * lat_cols
    row_c = lax.broadcasted_iota(jnp.int32, (cell_r, tile_c), 0).astype(F32)
    lane_c = lax.rem(lax.broadcasted_iota(jnp.int32, (cell_r, tile_c), 1), cell_c).astype(F32)
    for q in range(per_row):
        pick = jnp.where(wide_l == wide_c + q * BUMP_C, 1.0, 0.0).astype(jnp.bfloat16)
        flat = exact_pick([tall], pick)
        for i in range(seg_rows):
            lr = i * per_row + q
            rs = slice(lr * cell_r, (lr + 1) * cell_r)
            hit = (row_c == flat[i : i + 1, :]) & (
                lane_c == flat[seg_rows + i : seg_rows + i + 1, :]
            )
            m = jnp.where(hit, 1.0, 0.0)
            cm = m * flat[2 * seg_rows + i : 2 * seg_rows + i + 1, :]
            dg = 4.0 + shunt_ref[rs, :] + cm
            iv = 1.0 / dg
            mask[rs, :] = m
            diag[rs, :] = dg
            invd[rs, :] = iv
            cinv[rs, :] = cm * iv
    first = me * local_n
    mine_l = lax.broadcasted_iota(jnp.int32, (128, local_n), 0)
    mine_n = lax.broadcasted_iota(jnp.int32, (128, local_n), 1) + lax.rem(first, 128)
    own = jnp.broadcast_to(cond_ref[pl.ds(first // 128, 1), :], (8, 128))
    chere = exact_pick([own], jnp.where(mine_l == mine_n, 1.0, 0.0).astype(jnp.bfloat16))[0:1]

    bd[...] = jnp.zeros_like(bd)
    for q in range(local_n // PB):
        bd[q * PB : (q + 1) * PB, q * PB : (q + 1) * PB] = inv_ref[q]

    node_c = icol * lat_cols + lax.broadcasted_iota(jnp.int32, (tile_c, local_n), 0) // cell_c
    node_l = lax.broadcasted_iota(jnp.int32, (tile_c, local_n), 1)
    node_ct = icol * lat_cols + lax.broadcasted_iota(jnp.int32, (local_n, tile_c), 1) // cell_c
    node_lt = lax.broadcasted_iota(jnp.int32, (local_n, tile_c), 0)
    for g, (off, members) in enumerate(groups):
        emb[g] = jnp.where(node_c + off == node_l, 1.0, 0.0).astype(jnp.bfloat16)
        embt[g] = jnp.where(node_ct + off == node_lt, 1.0, 0.0).astype(jnp.bfloat16)

    lane_e = lax.broadcasted_iota(jnp.int32, (tile_r, 128), 1)
    row_i = lax.broadcasted_iota(jnp.int32, (tile_r, tile_c), 0)
    lane_i = lax.broadcasted_iota(jnp.int32, (tile_r, tile_c), 1)
    sub_k = lax.broadcasted_iota(jnp.int32, (batch, 128), 0)
    lane_k = lax.broadcasted_iota(jnp.int32, (batch, 128), 1)

    def remote(src, dst, ssem, rsem, r, c):
        return pltpu.make_async_remote_copy(
            src_ref=src, dst_ref=dst, send_sem=ssem, recv_sem=rsem,
            device_id=(r, c), device_id_type=MESH,
        )

    has = (irow > 0, irow < nrows - 1, icol > 0, icol < ncols - 1)

    def halos(it):
        return (
            remote(rsend.at[it, 0], hr.at[it, 1], hsend.at[it, 0], hrecv.at[it, 1], irow - 1, icol),
            remote(rsend.at[it, 1], hr.at[it, 0], hsend.at[it, 1], hrecv.at[it, 0], irow + 1, icol),
            remote(csend.at[it, 0], hc.at[it, 1], hsend.at[it, 2], hrecv.at[it, 3], irow, icol - 1),
            remote(csend.at[it, 1], hc.at[it, 0], hsend.at[it, 3], hrecv.at[it, 2], irow, icol + 1),
        )

    def put(slot, value):
        cf[slot] = jnp.broadcast_to(value, (batch, tile_c))

    def precond(v):
        return lax.dot_general(v, bd[...], (((1,), (1,)), ((), ())), precision=HI)

    def send_seg(it, v):
        seg[it, icol] = v
        for d in range(1, ncols):
            remote(
                seg.at[it, icol], seg.at[it, icol], ssend.at[it], srecv.at[it],
                irow, lax.rem(icol + d, ncols),
            ).start()

    def edges(it, k, v, e):
        one = pl.ds(k, 1)
        rsend[it, 0, one, :] = v[0:1, :]
        rsend[it, 1, one, :] = v[tile_r - 1 : tile_r, :]
        mv = v * mask[...]
        for lr in range(lat_rows):
            abuf[lr, one, :] = jnp.sum(mv[lr * cell_r : (lr + 1) * cell_r], axis=0, keepdims=True)
        e = jnp.where(lane_e == k, v[:, 0:1], e)
        return jnp.where(lane_e == k + batch, v[:, tile_c - 1 : tile_c], e)

    def send_edges(it, e):
        et = e.T
        csend[it, 0] = et[0:batch, :]
        csend[it, 1] = et[batch : 2 * batch, :]
        for side, copy in enumerate(halos(it)):
            pl.when(has[side])(copy.start)

    def send_cont(it):
        totals = [None] * ncols
        for g, (off, members) in enumerate(groups):
            out = exact_pick([abuf[lr] for lr, j in members], emb[g])
            for i, (lr, j) in enumerate(members):
                term = out[i * batch : (i + 1) * batch]
                totals[j] = term if totals[j] is None else totals[j] + term
        for j in range(ncols):
            cont[it, j] = totals[j]
        dat[it, icol] = cont[it, icol]
        for d in range(1, ncols):
            t = lax.rem(icol + d, ncols)
            remote(
                cont.at[it, t], dat.at[it, icol], csendm.at[it], drecv.at[it], irow, t
            ).start()

    def package_product(it):
        drain(seg.at[it, 0 : ncols - 1], srecv.at[it])
        acc = None
        for j in range(ncols):
            v = seg[it, j]
            vh = v.astype(jnp.bfloat16)
            vl = (v - vh.astype(F32)).astype(jnp.bfloat16)
            span = slice(j * local_n, (j + 1) * local_n)
            both = jnp.dot(
                jnp.concatenate([vh, vl], axis=0), mh[span, :], preferred_element_type=F32
            )
            term = both[:batch] + both[batch:]
            term += jnp.dot(vh, ml[span, :], preferred_element_type=F32)
            acc = term if acc is None else acc + term
        for m in range(nrows):
            part[it, m] = acc[:, m * local_n : (m + 1) * local_n]
        for m in range(nrows):
            n = icol * nrows + m
            copy = remote(
                part.at[it, m], rec.at[it, irow], psend.at[it], precv.at[it],
                n // ncols, lax.rem(n, ncols),
            )
            pl.when(n != me)(copy.start)

            @pl.when(n == me)
            def _():
                pltpu.make_async_copy(part.at[it, m], rec.at[it, irow], precv.at[it]).start()

        totals = [None] * lat_rows
        for g, (off, members) in enumerate(groups):
            out = exact_pick([seg[it, j] for lr, j in members], embt[g])
            for i, (lr, j) in enumerate(members):
                term = out[i * batch : (i + 1) * batch]
                totals[lr] = term if totals[lr] is None else totals[lr] + term
        for lr in range(lat_rows):
            vpx[lr] = totals[lr]

    def wait_halos(it):
        for side, index in enumerate(((hr, 0), (hr, 1), (hc, 0), (hc, 1))):
            ref, pos = index

            @pl.when(has[side])
            def _():
                drain(ref.at[it, pos], hrecv.at[it, side])

        return jnp.concatenate(
            [hc[it, 0], hc[it, 1], jnp.zeros((128 - 2 * batch, tile_r), F32)], axis=0
        ).T

    def image(it, k, v, ct):
        one = pl.ds(k, 1)
        left = jnp.sum(jnp.where(lane_e == k, ct, 0.0), axis=1, keepdims=True)
        right = jnp.sum(jnp.where(lane_e == k + batch, ct, 0.0), axis=1, keepdims=True)
        near = jnp.where(row_i == 0, hr[it, 0, one, :], pltpu.roll(v, 1, 0))
        near += jnp.where(row_i == tile_r - 1, hr[it, 1, one, :], pltpu.roll(v, tile_r - 1, 0))
        near += jnp.where(lane_i == 0, left, pltpu.roll(v, 1, 1))
        near += jnp.where(lane_i == tile_c - 1, right, pltpu.roll(v, tile_c - 1, 1))
        feed = jnp.concatenate(
            [
                cinv[lr * cell_r : (lr + 1) * cell_r, :] * vpx[lr, one, :]
                for lr in range(lat_rows)
            ],
            axis=0,
        )
        return v - near * invd[...] - feed

    def package_image(it, v):
        drain(rec.at[it], precv.at[it])
        drain(dat.at[it, 0 : ncols - 1], drecv.at[it])
        out = rec[it, 0]
        for i in range(1, nrows):
            out += rec[it, i]
        die_at = dat[it, 0]
        for j in range(1, ncols):
            die_at += dat[it, j]
        return out + chere * (v - die_at)

    def total(buf, a, b):
        return jnp.sum(buf[...], axis=1, keepdims=True) + jnp.sum(a * b, axis=1, keepdims=True)

    def send_sums(it, g, d):
        line = jnp.where(lane_k == sub_k, g, 0.0) + jnp.where(lane_k == sub_k + batch, d, 0.0)
        red[it, me] = jnp.sum(line, axis=0, keepdims=True)

        def spread(d, c):
            t = lax.rem(me + d, ndev)
            remote(
                red.at[it, me], red.at[it, me], rsendm.at[it], rrecv.at[it],
                t // ncols, lax.rem(t, ncols),
            ).start()
            return c

        lax.fori_loop(1, ndev, spread, 0)

    def take_sums(it):
        drain(red.at[it, 0 : ndev - 1], rrecv.at[it])
        line = jnp.sum(red[it], axis=0)
        g = jnp.sum(jnp.where(lane_k == sub_k, line, 0.0), axis=1, keepdims=True)
        d = jnp.sum(jnp.where(lane_k == sub_k + batch, line, 0.0), axis=1, keepdims=True)
        return g, d

    no_edges = jnp.zeros((tile_r, 128), F32)

    r0 = rp_ref[...]
    pu0 = precond(r0)
    pl.semaphore_wait(barrier, ndev - 1)
    send_seg(0, pu0)
    load_rd.wait()

    def start(k, e):
        r = rd_ref[k]
        u = r * invd[...]
        us[0, k] = u
        gbuf[pl.ds(k, 1), :] = jnp.sum(r * u, axis=0, keepdims=True)
        return edges(0, k, u, e)

    send_edges(0, lax.fori_loop(0, batch, start, no_edges))
    send_cont(0)
    load_mat.wait()
    high = mat_ref[...].astype(jnp.bfloat16)
    mh[...] = high
    ml[...] = (mat_ref[...] - high.astype(F32)).astype(jnp.bfloat16)

    package_product(0)
    ct0 = wait_halos(0)

    def first_image(k, e):
        u = us[0, k]
        m = image(0, k, u, ct0)
        ms[0, k] = m
        dbuf[pl.ds(k, 1), :] = jnp.sum(diag[...] * (m * u), axis=0, keepdims=True)
        return edges(1, k, m, e)

    e1 = lax.fori_loop(0, batch, first_image, no_edges)
    pw0 = package_image(0, pu0)
    pm0 = precond(pw0)
    send_seg(1, pm0)
    send_edges(1, e1)
    send_sums(0, total(gbuf, r0, pu0), total(dbuf, pw0, pu0))
    send_cont(1)

    package_product(1)
    ct1 = wait_halos(1)

    def second_image(k, c):
        ks[0, k] = image(1, k, ms[0, k], ct1)
        return c

    lax.fori_loop(0, batch, second_image, 0)
    pn0 = package_image(1, pm0)
    g0, d0 = take_sums(0)
    alpha0 = g0 / d0
    put(0, alpha0)
    pu1 = pu0 - alpha0 * pm0
    pw1 = pw0 - alpha0 * pn0
    r1 = r0 - alpha0 * pw0
    pm1 = precond(pw1)
    send_seg(2, pm1)

    def second_step(k, e):
        one = pl.ds(k, 1)
        a = cf[0, one, :]
        u = us[0, k] - a * ms[0, k]
        m = ms[0, k] - a * ks[0, k]
        us[1, k] = u
        ms[1, k] = m
        du = diag[...] * u
        gbuf[one, :] = jnp.sum(du * u, axis=0, keepdims=True)
        dbuf[one, :] = jnp.sum(du * m, axis=0, keepdims=True)
        return edges(2, k, m, e)

    e2 = lax.fori_loop(0, batch, second_step, no_edges)
    send_edges(2, e2)
    send_sums(1, total(gbuf, r1, pu1), total(dbuf, pw1, pu1))
    send_cont(2)

    package_product(2)
    ct2 = wait_halos(2)
    g1, d1 = take_sums(1)
    beta1 = g1 / g0
    alpha1 = g1 / (d1 - beta1 * g1 / alpha0)
    put(1, alpha1)
    put(2, beta1)

    def last_step(k, c):
        one = pl.ds(k, 1)
        a = cf[1, one, :]
        b = cf[2, one, :]
        m1 = ms[1, k]
        n = image(2, k, m1, ct2) + b * ks[0, k]
        u = us[1, k] - a * (m1 + b * ms[0, k])
        m = m1 - a * n
        us[2, k] = u
        du = diag[...] * u
        gbuf[one, :] = jnp.sum(du * u, axis=0, keepdims=True)
        dbuf[one, :] = jnp.sum(du * m, axis=0, keepdims=True)
        return c

    lax.fori_loop(0, batch, last_step, 0)
    pn1 = package_image(2, pm1)
    pu2 = pu1 - alpha1 * (pm1 + beta1 * pm0)
    pw2 = pw1 - alpha1 * (pn1 + beta1 * pn0)
    r2 = r1 - alpha1 * (pw1 + beta1 * pw0)
    send_sums(2, total(gbuf, r2, pu2), total(dbuf, pw2, pu2))

    mine = me // nrows == icol
    for it in range(ITERS):
        drain(seg.at[it, 0 : ncols - 1], ssend.at[it])
        drain(cont.at[it, 0 : ncols - 1], csendm.at[it])

        @pl.when(mine)
        def _():
            drain(part.at[it, 0 : nrows - 1], psend.at[it])

        @pl.when(jnp.logical_not(mine))
        def _():
            drain(part.at[it], psend.at[it])

        for side, copy in enumerate(halos(it)):
            pl.when(has[side])(copy.wait_send)

    g2, d2 = take_sums(2)
    beta2 = g2 / g1
    c2 = g2 / (d2 - beta2 * g2 / alpha1)
    c1 = alpha1 + c2 * beta2
    c0 = alpha0 + c1 * beta1
    put(0, c0)
    put(1, c1)
    put(2, c2)
    xp_ref[...] = c0 * pu0 + c1 * pu1 + c2 * pu2

    def finish(k, c):
        one = pl.ds(k, 1)
        xd_ref[k] = cf[0, one, :] * us[0, k] + cf[1, one, :] * us[1, k] + cf[2, one, :] * us[2, k]
        return c

    lax.fori_loop(0, batch, finish, 0)
    for it in range(ITERS):
        drain(red.at[it, 0 : ndev - 1], rsendm.at[it])


def solution(mesh):
    nrows, ncols = mesh.shape["row"], mesh.shape["col"]

    def body(die_current, die_shunt, pkg_current, pkg_matrix, pkg_block_inv, bump_node, bump_conductance):
        batch, tile_r, tile_c = die_current.shape
        local_n = pkg_current.shape[1]
        bumps = bump_node.shape[0]
        lat_rows = bumps // BUMP_C // nrows
        lat_cols = BUMP_C // ncols
        nodes = bump_node.reshape(-1, 128)
        cond = bump_conductance.reshape(-1, 128)
        noff = len(pairs_by_offset(lat_rows, ncols, local_n))
        ndev = nrows * ncols
        vm = pltpu.VMEM
        dma = pltpu.SemaphoreType.DMA
        row = (batch, tile_c)
        return pl.pallas_call(
            functools.partial(kernel, nrows, ncols, lat_rows, lat_cols),
            out_shape=(
                jax.ShapeDtypeStruct(die_current.shape, F32),
                jax.ShapeDtypeStruct(pkg_current.shape, F32),
            ),
            in_specs=[
                pl.BlockSpec(memory_space=pltpu.HBM if i in (0, 3) else pltpu.VMEM)
                for i in range(7)
            ],
            out_specs=(pl.BlockSpec(memory_space=pltpu.VMEM),) * 2,
            scratch_shapes=[
                vm(die_current.shape, F32),
                vm(pkg_matrix.shape, F32),
                vm((3,) + die_current.shape, F32),
                vm((2,) + die_current.shape, F32),
                vm((1,) + die_current.shape, F32),
                vm((tile_r, tile_c), F32),
                vm((tile_r, tile_c), F32),
                vm((tile_r, tile_c), F32),
                vm((tile_r, tile_c), F32),
                vm(pkg_matrix.shape, jnp.bfloat16),
                vm(pkg_matrix.shape, jnp.bfloat16),
                vm((local_n, local_n), F32),
                vm(row, F32),
                vm(row, F32),
                vm((3,) + row, F32),
                vm((lat_rows,) + row, F32),
                vm((lat_rows,) + row, F32),
                vm((noff, tile_c, local_n), jnp.bfloat16),
                vm((noff, local_n, tile_c), jnp.bfloat16),
                vm((ITERS, 2) + row, F32),
                vm((ITERS, 2) + row, F32),
                vm((ITERS, 2, batch, tile_r), F32),
                vm((ITERS, 2, batch, tile_r), F32),
                vm((ITERS, ncols, batch, local_n), F32),
                vm((ITERS, nrows, batch, local_n), F32),
                vm((ITERS, nrows, batch, local_n), F32),
                vm((ITERS, ncols, batch, local_n), F32),
                vm((ITERS, ncols, batch, local_n), F32),
                vm((ITERS, ndev, 1, 128), F32),
                dma((ITERS, 4)),
                dma((ITERS, 4)),
                dma((ITERS,)),
                dma((ITERS,)),
                dma((ITERS,)),
                dma((ITERS,)),
                dma((ITERS,)),
                dma((ITERS,)),
                dma((ITERS,)),
                dma((ITERS,)),
                dma((2,)),
            ],
            compiler_params=pltpu.CompilerParams(
                collective_id=0, has_side_effects=True, vmem_limit_bytes=48 << 20
            ),
        )(die_current, die_shunt, pkg_current, pkg_matrix, pkg_block_inv, nodes, cond)

    placed = (
        P(None, "row", "col"),
        P("row", "col"),
        P(None, ("row", "col")),
        P("row", "col"),
        P(("row", "col"), None, None),
        P(),
        P(),
    )
    return jax.shard_map(
        body,
        mesh=mesh,
        in_specs=placed,
        out_specs=(P(None, "row", "col"), P(None, ("row", "col"))),
        check_vma=False,
    )
```

time: 60.3 us -> 49.7 us (0.82)
  Pallas kernels: 50.4 us -> 41.2 us
  local copies, waits for them, and re-layouts: 8.77 us -> 7.38 us
    pallas_call x1, Pallas kernels: 50.4 us -> 41.2 us  [body(): pl.pallas_call(functools.partial(kernel, nrows, ncols, lat_rows, lat_cols...]
    reshape x5 -> x0, local copies, waits for them, and re-layouts: 2.52 us -> none  [the longest x1 0.79 us: body(): bump_conductance.reshape(-1, BUMP_C)]
    unnamed x10 -> x14, local copies, waits for them, and re-layouts: 5.94 us -> 7.38 us
where the time goes in v2:
time: 49.7 us; the launch traced here: 49.3 us
  Pallas kernels  41.2 us (83%)
  local copies, waits for them, and re-layouts  7.38 us (15%)
  between operations  0.65 us (1%)
    pallas_call x1, Pallas kernels, body(): pl.pallas_call(functools.partial(kernel, nrows, ncols, lat_rows, lat_cols...  41.2 us
    unnamed x14, local copies, waits for them, and re-layouts  7.38 us

profile of v2, /device:TPU:0, one launch (start us, length us, event | category | flops | bytes accessed | tf_op | source)
XLA Modules:
  0.0 49.3 jit_solution(2074999727260694782)
XLA Ops:
  0.6 0.0 copy-start
  0.6 1.6 %copy-done = f32[16,128,256]{2,1,0:T(8,128)S(1)} copy-done((f32[16,128,256]{2,1,0:T(8,128)S(1)}, f32[16,128,256]{2,1,0:T(8,128)}, u32[]{:S(2)}) %copy-start) | copy-done | bytes 2097176
  2.2 0.0 copy-start.1
  2.2 0.9 %copy-done.1 = f32[128,256]{1,0:T(8,128)S(1)} copy-done((f32[128,256]{1,0:T(8,128)S(1)}, f32[128,256]{1,0:T(8,128)}, u32[]{:S(2)}) %copy-start.1) | copy-done | bytes 131096
  3.1 0.0 copy-start.2
  3.1 0.8 %copy-done.2 = f32[4,32,32]{2,1,0:T(8,128)S(1)} copy-done((f32[4,32,32]{2,1,0:T(8,128)S(1)}, f32[4,32,32]{2,1,0:T(8,128)}, u32[]{:S(2)}) %copy-start.2) | copy-done | bytes 16408
  4.0 0.0 copy-start.3
  4.0 0.7 %copy-done.3 = s32[4096]{0:T(1024)S(1)} copy-done((s32[4096]{0:T(1024)S(1)}, s32[4096]{0:T(1024)}, u32[]{:S(2)}) %copy-start.3) | copy-done | bytes 16408
  4.7 0.0 copy-start.4
  4.7 0.7 %copy-done.4 = f32[4096]{0:T(1024)S(1)} copy-done((f32[4096]{0:T(1024)S(1)}, f32[4096]{0:T(1024)}, u32[]{:S(2)}) %copy-start.4) | copy-done | bytes 16408
  5.4 0.0 copy-start.5
  5.4 0.7 %copy-done.5 = f32[16,128]{1,0:T(8,128)S(1)} copy-done((f32[16,128]{1,0:T(8,128)S(1)}, f32[16,128]{1,0:T(8,128)}, u32[]{:S(2)}) %copy-start.5) | copy-done | bytes 8216
  6.1 41.2 %shard_map.86 = (f32[16,128,256]{2,1,0:T(8,128)S(1)}, f32[16,128]{1,0:T(8,128)S(1)}) custom-call(f32[16,128,256]{2,1,0:T(8,128)S(1)} %copy-done, f32[128,256]{1,0:T(8,128)S(1)} %copy-done.1, f32[16,128]{1,0:T(8,128)S(1)} %copy-done.5, f32[512,1024]{1,0:T(8,128)} %mat_hbm.1, f32[4,32,32]{2,1,0:T(8,128)S(1)} %copy-done.2, s32[32,128]{1,0:T(8,128)S(1)} %bitcast.2, ...), custom_call_target="tpu_custom_call" | custom-call | tf_op jit(solution)/shard_map/pallas_call | solution.py:457
  47.3 1.3 %copy.11 = f32[16,128,256]{2,1,0:T(8,128)} copy(f32[16,128,256]{2,1,0:T(8,128)S(1)} %get-tuple-element.4) | data formatting | bytes 4194304
  48.7 0.6 %copy.12 = f32[16,128]{1,0:T(8,128)} copy(f32[16,128]{1,0:T(8,128)S(1)} %get-tuple-element.5) | data formatting | bytes 16384
Async XLA Ops:
  0.6 1.6 %copy-start = (f32[16,128,256]{2,1,0:T(8,128)S(1)}, f32[16,128,256]{2,1,0:T(8,128)}, u32[]{:S(2)}) copy-start(f32[16,128,256]{2,1,0:T(8,128)} %rd_hbm.1) | copy-start | bytes 6291460
  2.2 0.9 %copy-start.1 = (f32[128,256]{1,0:T(8,128)S(1)}, f32[128,256]{1,0:T(8,128)}, u32[]{:S(2)}) copy-start(f32[128,256]{1,0:T(8,128)} %shunt_ref.1) | copy-start | bytes 393220
  3.1 0.8 %copy-start.2 = (f32[4,32,32]{2,1,0:T(8,128)S(1)}, f32[4,32,32]{2,1,0:T(8,128)}, u32[]{:S(2)}) copy-start(f32[4,32,32]{2,1,0:T(8,128)} %inv_ref.1) | copy-start | bytes 49156
  4.0 0.7 %copy-start.3 = (s32[4096]{0:T(1024)S(1)}, s32[4096]{0:T(1024)}, u32[]{:S(2)}) copy-start(s32[4096]{0:T(1024)} %param.12) | copy-start | bytes 49156
  4.7 0.7 %copy-start.4 = (f32[4096]{0:T(1024)S(1)}, f32[4096]{0:T(1024)}, u32[]{:S(2)}) copy-start(f32[4096]{0:T(1024)} %param.13) | copy-start | bytes 49156
  5.4 0.7 %copy-start.5 = (f32[16,128]{1,0:T(8,128)S(1)}, f32[16,128]{1,0:T(8,128)}, u32[]{:S(2)}) copy-start(f32[16,128]{1,0:T(8,128)} %rp_ref.1) | copy-start | bytes 24580

commit v3 on v2

--- a/solution.py
+++ b/solution.py
@@ -46,11 +46,11 @@
 
 def kernel(
     nrows, ncols, lat_rows, lat_cols,
-    rd_hbm, shunt_ref, rp_ref, mat_hbm, inv_ref, node_ref, cond_ref,
-    xd_ref, xp_ref,
-    rd_ref, mat_ref, us, ms, ks, diag, invd, mask, cinv, mh, ml, bd, gbuf, dbuf, cf, abuf, vpx,
+    rd_hbm, shunt_hbm, rp_hbm, mat_hbm, inv_hbm, node_hbm, cond_hbm,
+    xd_hbm, xp_hbm,
+    rd_ref, mat_ref, shunt_ref, rp_ref, inv_ref, node_ref, cond_ref, xp_ref, us, ms, ks, diag, invd, mask, cinv, mh, ml, bd, gbuf, dbuf, cf, abuf, vpx,
     emb, embt, rsend, hr, csend, hc, seg, part, rec, cont, dat, red,
-    hsend, hrecv, ssend, srecv, psend, precv, csendm, drecv, rsendm, rrecv, loadsem,
+    hsend, hrecv, ssend, srecv, psend, precv, csendm, drecv, rsendm, rrecv, loadsem, outsem,
 ):
     ndev = nrows * ncols
     irow = lax.axis_index("row")
@@ -63,10 +63,22 @@
     total_c = tile_c * ncols
     groups = pairs_by_offset(lat_rows, ncols, local_n)
 
-    load_rd = pltpu.make_async_copy(rd_hbm, rd_ref, loadsem.at[0])
-    load_mat = pltpu.make_async_copy(mat_hbm, mat_ref, loadsem.at[1])
-    load_rd.start()
-    load_mat.start()
+    loads = [
+        pltpu.make_async_copy(src, dst, loadsem.at[i])
+        for i, (src, dst) in enumerate(
+            (
+                (node_hbm, node_ref),
+                (cond_hbm, cond_ref),
+                (shunt_hbm, shunt_ref),
+                (inv_hbm, inv_ref),
+                (rp_hbm, rp_ref),
+                (rd_hbm, rd_ref),
+                (mat_hbm, mat_ref),
+            )
+        )
+    ]
+    for load in loads:
+        load.start()
 
     hr[...] = jnp.zeros_like(hr)
     hc[...] = jnp.zeros_like(hc)
@@ -81,6 +93,17 @@
 
     lax.fori_loop(1, ndev, greet, 0)
 
+    node_c = icol * lat_cols + lax.broadcasted_iota(jnp.int32, (tile_c, local_n), 0) // cell_c
+    node_l = lax.broadcasted_iota(jnp.int32, (tile_c, local_n), 1)
+    node_ct = icol * lat_cols + lax.broadcasted_iota(jnp.int32, (local_n, tile_c), 1) // cell_c
+    node_lt = lax.broadcasted_iota(jnp.int32, (local_n, tile_c), 0)
+    for g, (off, members) in enumerate(groups):
+        emb[g] = jnp.where(node_c + off == node_l, 1.0, 0.0).astype(jnp.bfloat16)
+        embt[g] = jnp.where(node_ct + off == node_lt, 1.0, 0.0).astype(jnp.bfloat16)
+    bd[...] = jnp.zeros_like(bd)
+
+    for load in loads[:5]:
+        load.wait()
     seg_rows = lat_rows * BUMP_C // 128
     per_row = 128 // BUMP_C
     nodes = node_ref[pl.ds(irow * seg_rows, seg_rows), :]
@@ -116,17 +139,8 @@
     own = jnp.broadcast_to(cond_ref[pl.ds(first // 128, 1), :], (8, 128))
     chere = exact_pick([own], jnp.where(mine_l == mine_n, 1.0, 0.0).astype(jnp.bfloat16))[0:1]
 
-    bd[...] = jnp.zeros_like(bd)
     for q in range(local_n // PB):
         bd[q * PB : (q + 1) * PB, q * PB : (q + 1) * PB] = inv_ref[q]
-
-    node_c = icol * lat_cols + lax.broadcasted_iota(jnp.int32, (tile_c, local_n), 0) // cell_c
-    node_l = lax.broadcasted_iota(jnp.int32, (tile_c, local_n), 1)
-    node_ct = icol * lat_cols + lax.broadcasted_iota(jnp.int32, (local_n, tile_c), 1) // cell_c
-    node_lt = lax.broadcasted_iota(jnp.int32, (local_n, tile_c), 0)
-    for g, (off, members) in enumerate(groups):
-        emb[g] = jnp.where(node_c + off == node_l, 1.0, 0.0).astype(jnp.bfloat16)
-        embt[g] = jnp.where(node_ct + off == node_lt, 1.0, 0.0).astype(jnp.bfloat16)
 
     lane_e = lax.broadcasted_iota(jnp.int32, (tile_r, 128), 1)
     row_i = lax.broadcasted_iota(jnp.int32, (tile_r, tile_c), 0)
@@ -304,7 +318,7 @@
     pu0 = precond(r0)
     pl.semaphore_wait(barrier, ndev - 1)
     send_seg(0, pu0)
-    load_rd.wait()
+    loads[5].wait()
 
     def start(k, e):
         r = rd_ref[k]
@@ -315,7 +329,7 @@
 
     send_edges(0, lax.fori_loop(0, batch, start, no_edges))
     send_cont(0)
-    load_mat.wait()
+    loads[6].wait()
     high = mat_ref[...].astype(jnp.bfloat16)
     mh[...] = high
     ml[...] = (mat_ref[...] - high.astype(F32)).astype(jnp.bfloat16)
@@ -375,6 +389,12 @@
 
     package_product(2)
     ct2 = wait_halos(2)
+
+    def third_image(k, c):
+        ks[1, k] = image(2, k, ms[1, k], ct2)
+        return c
+
+    lax.fori_loop(0, batch, third_image, 0)
     g1, d1 = take_sums(1)
     beta1 = g1 / g0
     alpha1 = g1 / (d1 - beta1 * g1 / alpha0)
@@ -386,9 +406,8 @@
         a = cf[1, one, :]
         b = cf[2, one, :]
         m1 = ms[1, k]
-        n = image(2, k, m1, ct2) + b * ks[0, k]
         u = us[1, k] - a * (m1 + b * ms[0, k])
-        m = m1 - a * n
+        m = m1 - a * (ks[1, k] + b * ks[0, k])
         us[2, k] = u
         du = diag[...] * u
         gbuf[one, :] = jnp.sum(du * u, axis=0, keepdims=True)
@@ -427,13 +446,18 @@
     put(1, c1)
     put(2, c2)
     xp_ref[...] = c0 * pu0 + c1 * pu1 + c2 * pu2
+    xp_out = pltpu.make_async_copy(xp_ref, xp_hbm, outsem.at[0])
+    xp_out.start()
 
     def finish(k, c):
         one = pl.ds(k, 1)
-        xd_ref[k] = cf[0, one, :] * us[0, k] + cf[1, one, :] * us[1, k] + cf[2, one, :] * us[2, k]
+        rd_ref[k] = cf[0, one, :] * us[0, k] + cf[1, one, :] * us[1, k] + cf[2, one, :] * us[2, k]
+        pltpu.make_async_copy(rd_ref.at[k], xd_hbm.at[k], outsem.at[1]).start()
         return c
 
     lax.fori_loop(0, batch, finish, 0)
+    xp_out.wait()
+    pltpu.make_async_copy(rd_ref, xd_hbm, outsem.at[1]).wait()
     for it in range(ITERS):
         drain(red.at[it, 0 : ndev - 1], rsendm.at[it])
 
@@ -460,17 +484,20 @@
                 jax.ShapeDtypeStruct(die_current.shape, F32),
                 jax.ShapeDtypeStruct(pkg_current.shape, F32),
             ),
-            in_specs=[
-                pl.BlockSpec(memory_space=pltpu.HBM if i in (0, 3) else pltpu.VMEM)
-                for i in range(7)
-            ],
-            out_specs=(pl.BlockSpec(memory_space=pltpu.VMEM),) * 2,
+            in_specs=[pl.BlockSpec(memory_space=pltpu.HBM)] * 7,
+            out_specs=(pl.BlockSpec(memory_space=pltpu.HBM),) * 2,
             scratch_shapes=[
                 vm(die_current.shape, F32),
                 vm(pkg_matrix.shape, F32),
+                vm(die_shunt.shape, F32),
+                vm(pkg_current.shape, F32),
+                vm(pkg_block_inv.shape, F32),
+                vm(nodes.shape, jnp.int32),
+                vm(cond.shape, F32),
+                vm(pkg_current.shape, F32),
                 vm((3,) + die_current.shape, F32),
                 vm((2,) + die_current.shape, F32),
-                vm((1,) + die_current.shape, F32),
+                vm((2,) + die_current.shape, F32),
                 vm((tile_r, tile_c), F32),
                 vm((tile_r, tile_c), F32),
                 vm((tile_r, tile_c), F32),
@@ -505,10 +532,11 @@
                 dma((ITERS,)),
                 dma((ITERS,)),
                 dma((ITERS,)),
+                dma((7,)),
                 dma((2,)),
             ],
             compiler_params=pltpu.CompilerParams(
-                collective_id=0, has_side_effects=True, vmem_limit_bytes=48 << 20
+                collective_id=0, has_side_effects=True, vmem_limit_bytes=67043328
             ),
         )(die_current, die_shunt, pkg_current, pkg_matrix, pkg_block_inv, nodes, cond)
 

time: 49.7 us -> 46.2 us (0.930)
  local copies, waits for them, and re-layouts: 7.38 us -> 3.7 us
  Pallas kernels: 41.2 us -> 41.7 us
    unnamed x14 -> x4, local copies, waits for them, and re-layouts: 7.38 us -> 3.7 us
where the time goes in v3:
time: 46.2 us; the launch traced here: 46 us
  Pallas kernels  41.7 us (90%)
  local copies, waits for them, and re-layouts  3.7 us (8%)
  between operations  0.65 us (1%)
    pallas_call x1, Pallas kernels, body(): pl.pallas_call(functools.partial(kernel, nrows, ncols, lat_rows, lat_cols...  41.7 us
    unnamed x4, local copies, waits for them, and re-layouts  3.7 us

profile of v3, /device:TPU:0, one launch (start us, length us, event | category | flops | bytes accessed | tf_op | source)
XLA Modules:
  0.0 46.0 jit_solution(18269951211865771673)
XLA Ops:
  0.6 41.7 %shard_map.86 = (f32[16,128,256]{2,1,0:T(8,128)}, f32[16,128]{1,0:T(8,128)}) custom-call(f32[16,128,256]{2,1,0:T(8,128)} %rd_hbm.1, f32[128,256]{1,0:T(8,128)} %shunt_hbm.1, f32[16,128]{1,0:T(8,128)} %rp_hbm.1, f32[512,1024]{1,0:T(8,128)} %mat_hbm.1, f32[4,32,32]{2,1,0:T(8,128)} %inv_hbm.1, s32[32,128]{1,0:T(8,128)} %bitcast.2, f32[32,128]{1,0:T(8,128)} %bitcast.3), custom_call_target="tpu_custom_call" | custom-call | tf_op jit(solution)/shard_map/pallas_call | solution.py:481
  42.3 0.0 copy-start
  42.3 3.1 %copy.11 = f32[16,128,256]{2,1,0:T(8,128)} copy(f32[16,128,256]{2,1,0:T(8,128)} %get-tuple-element.4) | data formatting | bytes 4194304
  45.4 0.0 copy-done
  45.4 0.6 %copy.12 = f32[16,128]{1,0:T(8,128)} copy(f32[16,128]{1,0:T(8,128)S(1)} %copy-done) | data formatting | bytes 16384
Async XLA Ops:
  42.3 3.1 %copy-start = (f32[16,128]{1,0:T(8,128)S(1)}, f32[16,128]{1,0:T(8,128)}, u32[]{:S(2)}) copy-start(f32[16,128]{1,0:T(8,128)} %get-tuple-element.5) | copy-start | bytes 24580

commit v4 on v3

--- a/solution.py
+++ b/solution.py
@@ -47,7 +47,7 @@
 def kernel(
     nrows, ncols, lat_rows, lat_cols,
     rd_hbm, shunt_hbm, rp_hbm, mat_hbm, inv_hbm, node_hbm, cond_hbm,
-    xd_hbm, xp_hbm,
+    us_hbm, cf_hbm, xp_hbm,
     rd_ref, mat_ref, shunt_ref, rp_ref, inv_ref, node_ref, cond_ref, xp_ref, us, ms, ks, diag, invd, mask, cinv, mh, ml, bd, gbuf, dbuf, cf, abuf, vpx,
     emb, embt, rsend, hr, csend, hc, seg, part, rec, cont, dat, red,
     hsend, hrecv, ssend, srecv, psend, precv, csendm, drecv, rsendm, rrecv, loadsem, outsem,
@@ -327,7 +327,9 @@
         gbuf[pl.ds(k, 1), :] = jnp.sum(r * u, axis=0, keepdims=True)
         return edges(0, k, u, e)
 
-    send_edges(0, lax.fori_loop(0, batch, start, no_edges))
+    send_edges(0, lax.fori_loop(0, batch, start, no_edges, unroll=2))
+    outs = [pltpu.make_async_copy(us.at[i], us_hbm.at[i], outsem.at[i]) for i in range(ITERS)]
+    outs[0].start()
     send_cont(0)
     loads[6].wait()
     high = mat_ref[...].astype(jnp.bfloat16)
@@ -359,7 +361,7 @@
         ks[0, k] = image(1, k, ms[0, k], ct1)
         return c
 
-    lax.fori_loop(0, batch, second_image, 0)
+    lax.fori_loop(0, batch, second_image, 0, unroll=2)
     pn0 = package_image(1, pm0)
     g0, d0 = take_sums(0)
     alpha0 = g0 / d0
@@ -382,8 +384,9 @@
         dbuf[one, :] = jnp.sum(du * m, axis=0, keepdims=True)
         return edges(2, k, m, e)
 
-    e2 = lax.fori_loop(0, batch, second_step, no_edges)
+    e2 = lax.fori_loop(0, batch, second_step, no_edges, unroll=2)
     send_edges(2, e2)
+    outs[1].start()
     send_sums(1, total(gbuf, r1, pu1), total(dbuf, pw1, pu1))
     send_cont(2)
 
@@ -394,7 +397,7 @@
         ks[1, k] = image(2, k, ms[1, k], ct2)
         return c
 
-    lax.fori_loop(0, batch, third_image, 0)
+    lax.fori_loop(0, batch, third_image, 0, unroll=2)
     g1, d1 = take_sums(1)
     beta1 = g1 / g0
     alpha1 = g1 / (d1 - beta1 * g1 / alpha0)
@@ -414,11 +417,12 @@
         dbuf[one, :] = jnp.sum(du * m, axis=0, keepdims=True)
         return c
 
-    lax.fori_loop(0, batch, last_step, 0)
+    lax.fori_loop(0, batch, last_step, 0, unroll=2)
     pn1 = package_image(2, pm1)
     pu2 = pu1 - alpha1 * (pm1 + beta1 * pm0)
     pw2 = pw1 - alpha1 * (pn1 + beta1 * pn0)
     r2 = r1 - alpha1 * (pw1 + beta1 * pw0)
+    outs[2].start()
     send_sums(2, total(gbuf, r2, pu2), total(dbuf, pw2, pu2))
 
     mine = me // nrows == icol
@@ -446,18 +450,12 @@
     put(1, c1)
     put(2, c2)
     xp_ref[...] = c0 * pu0 + c1 * pu1 + c2 * pu2
-    xp_out = pltpu.make_async_copy(xp_ref, xp_hbm, outsem.at[0])
-    xp_out.start()
-
-    def finish(k, c):
-        one = pl.ds(k, 1)
-        rd_ref[k] = cf[0, one, :] * us[0, k] + cf[1, one, :] * us[1, k] + cf[2, one, :] * us[2, k]
-        pltpu.make_async_copy(rd_ref.at[k], xd_hbm.at[k], outsem.at[1]).start()
-        return c
-
-    lax.fori_loop(0, batch, finish, 0)
-    xp_out.wait()
-    pltpu.make_async_copy(rd_ref, xd_hbm, outsem.at[1]).wait()
+    outs.append(pltpu.make_async_copy(xp_ref, xp_hbm, outsem.at[ITERS]))
+    outs.append(pltpu.make_async_copy(cf, cf_hbm, outsem.at[ITERS + 1]))
+    outs[ITERS].start()
+    outs[ITERS + 1].start()
+    for out in outs:
+        out.wait()
     for it in range(ITERS):
         drain(red.at[it, 0 : ndev - 1], rsendm.at[it])
 
@@ -478,14 +476,15 @@
         vm = pltpu.VMEM
         dma = pltpu.SemaphoreType.DMA
         row = (batch, tile_c)
-        return pl.pallas_call(
+        us, cf, xp = pl.pallas_call(
             functools.partial(kernel, nrows, ncols, lat_rows, lat_cols),
             out_shape=(
-                jax.ShapeDtypeStruct(die_current.shape, F32),
+                jax.ShapeDtypeStruct((ITERS,) + die_current.shape, F32),
+                jax.ShapeDtypeStruct((ITERS,) + row, F32),
                 jax.ShapeDtypeStruct(pkg_current.shape, F32),
             ),
             in_specs=[pl.BlockSpec(memory_space=pltpu.HBM)] * 7,
-            out_specs=(pl.BlockSpec(memory_space=pltpu.HBM),) * 2,
+            out_specs=(pl.BlockSpec(memory_space=pltpu.HBM),) * 3,
             scratch_shapes=[
                 vm(die_current.shape, F32),
                 vm(pkg_matrix.shape, F32),
@@ -533,12 +532,15 @@
                 dma((ITERS,)),
                 dma((ITERS,)),
                 dma((7,)),
-                dma((2,)),
+                dma((ITERS + 2,)),
             ],
             compiler_params=pltpu.CompilerParams(
                 collective_id=0, has_side_effects=True, vmem_limit_bytes=67043328
             ),
         )(die_current, die_shunt, pkg_current, pkg_matrix, pkg_block_inv, nodes, cond)
+        scale = cf[:, :, None, :]
+        xd = scale[0] * us[0] + scale[1] * us[1] + scale[2] * us[2]
+        return xd, xp
 
     placed = (
         P(None, "row", "col"),

time: 46.2 us -> 46.7 us (1.011)
  other arithmetic: 0 us -> 4.92 us
  local copies, waits for them, and re-layouts: 3.7 us -> 1.36 us
  Pallas kernels: 41.7 us -> 39.4 us
    add x0 -> x1, other arithmetic: none -> 4.92 us  [body(): xd = scale[0] * us[0] + scale[1] * us[1] + scale[2] * us[2]]
    unnamed x4 -> x3, local copies, waits for them, and re-layouts: 3.7 us -> 0.6 us
    pallas_call x1, Pallas kernels: 41.7 us -> 39.4 us  [body(): pl.pallas_call(functools.partial(kernel, nrows, ncols, lat_rows, lat_cols...]
    mul x0 -> x1, local copies, waits for them, and re-layouts: none -> 0.76 us  [body(): xd = scale[0] * us[0] + scale[1] * us[1] + scale[2] * us[2]]
where the time goes in v4:
time: 46.7 us; the launch traced here: 46.3 us
  Pallas kernels  39.4 us (84%)
  other arithmetic  4.92 us (11%)
  local copies, waits for them, and re-layouts  1.36 us (3%)
  between operations  0.64 us (1%)
    pallas_call x1, Pallas kernels, body(): pl.pallas_call(functools.partial(kernel, nrows, ncols, lat_rows, lat_cols...  39.4 us
    add x1, other arithmetic, body(): xd = scale[0] * us[0] + scale[1] * us[1] + scale[2] * us[2]  4.92 us

profile of v4, /device:TPU:0, one launch (start us, length us, event | category | flops | bytes accessed | tf_op | source)
XLA Modules:
  0.0 46.3 jit_solution(13249684630454763274)
XLA Ops:
  0.6 39.4 %shard_map.86 = (f32[3,16,128,256]{3,2,1,0:T(8,128)}, f32[3,16,256]{2,1,0:T(8,128)}, f32[16,128]{1,0:T(8,128)}) custom-call(f32[16,128,256]{2,1,0:T(8,128)} %rd_hbm.1, f32[128,256]{1,0:T(8,128)} %shunt_hbm.1, f32[16,128]{1,0:T(8,128)} %rp_hbm.1, f32[512,1024]{1,0:T(8,128)} %mat_hbm.1, f32[4,32,32]{2,1,0:T(8,128)} %inv_hbm.1, s32[32,128]{1,0:T(8,128)} %bitcast.22, ...), custom_call_target="tpu_custom_call" | custom-call | tf_op jit(solution)/shard_map/pallas_call | solution.py:479
  40.1 0.8 %slice_bitcast_fusion.2 = (f32[16,256]{1,0:T(8,128)S(1)}, f32[16,256]{1,0:T(8,128)S(1)}, f32[16,256]{1,0:T(8,128)S(1)}) fusion(f32[3,16,256]{2,1,0:T(8,128)} %get-tuple-element.5), kind=kLoop, calls=%fused_computation.7 | loop fusion | bytes 98304 | tf_op jit(solution)/shard_map/mul | solution.py:542
  40.8 0.0 copy-start
  40.8 4.9 %fusion = f32[16,128,256]{2,1,0:T(8,128)} fusion(f32[3,16,128,256]{3,2,1,0:T(8,128)} %get-tuple-element.6, f32[16,256]{1,0:T(8,128)S(1)} %get-tuple-element.9, f32[16,256]{1,0:T(8,128)S(1)} %get-tuple-element.10, f32[16,256]{1,0:T(8,128)S(1)} %get-tuple-element.8), kind=kLoop, calls=%fused_computation.1 | loop fusion | flops 2621440 | bytes 8437760 | tf_op jit(solution)/shard_map/add | solution.py:542
  45.7 0.0 copy-done
  45.7 0.6 %copy.10 = f32[16,128]{1,0:T(8,128)} copy(f32[16,128]{1,0:T(8,128)S(1)} %copy-done) | data formatting | bytes 16384
Async XLA Ops:
  40.8 4.9 %copy-start = (f32[16,128]{1,0:T(8,128)S(1)}, f32[16,128]{1,0:T(8,128)}, u32[]{:S(2)}) copy-start(f32[16,128]{1,0:T(8,128)} %get-tuple-element.14) | copy-start | bytes 24580

commit v5 on v3

--- a/solution.py
+++ b/solution.py
@@ -327,7 +327,7 @@
         gbuf[pl.ds(k, 1), :] = jnp.sum(r * u, axis=0, keepdims=True)
         return edges(0, k, u, e)
 
-    send_edges(0, lax.fori_loop(0, batch, start, no_edges))
+    send_edges(0, lax.fori_loop(0, batch, start, no_edges, unroll=2))
     send_cont(0)
     loads[6].wait()
     high = mat_ref[...].astype(jnp.bfloat16)
@@ -359,7 +359,7 @@
         ks[0, k] = image(1, k, ms[0, k], ct1)
         return c
 
-    lax.fori_loop(0, batch, second_image, 0)
+    lax.fori_loop(0, batch, second_image, 0, unroll=2)
     pn0 = package_image(1, pm0)
     g0, d0 = take_sums(0)
     alpha0 = g0 / d0
@@ -382,7 +382,7 @@
         dbuf[one, :] = jnp.sum(du * m, axis=0, keepdims=True)
         return edges(2, k, m, e)
 
-    e2 = lax.fori_loop(0, batch, second_step, no_edges)
+    e2 = lax.fori_loop(0, batch, second_step, no_edges, unroll=2)
     send_edges(2, e2)
     send_sums(1, total(gbuf, r1, pu1), total(dbuf, pw1, pu1))
     send_cont(2)
@@ -394,7 +394,7 @@
         ks[1, k] = image(2, k, ms[1, k], ct2)
         return c
 
-    lax.fori_loop(0, batch, third_image, 0)
+    lax.fori_loop(0, batch, third_image, 0, unroll=2)
     g1, d1 = take_sums(1)
     beta1 = g1 / g0
     alpha1 = g1 / (d1 - beta1 * g1 / alpha0)
@@ -414,7 +414,7 @@
         dbuf[one, :] = jnp.sum(du * m, axis=0, keepdims=True)
         return c
 
-    lax.fori_loop(0, batch, last_step, 0)
+    lax.fori_loop(0, batch, last_step, 0, unroll=2)
     pn1 = package_image(2, pm1)
     pu2 = pu1 - alpha1 * (pm1 + beta1 * pm0)
     pw2 = pw1 - alpha1 * (pn1 + beta1 * pn0)
@@ -460,6 +460,21 @@
     pltpu.make_async_copy(rd_ref, xd_hbm, outsem.at[1]).wait()
     for it in range(ITERS):
         drain(red.at[it, 0 : ndev - 1], rsendm.at[it])
+
+
+def deliver(x_hbm, p_hbm, xo_hbm, po_hbm, buf, pbuf, insem, outsem):
+    batch = buf.shape[0]
+    steps = [(x_hbm.at[k], buf.at[k], xo_hbm.at[k]) for k in range(batch)]
+    steps.append((p_hbm, pbuf, po_hbm))
+    ins = [pltpu.make_async_copy(a, b, insem.at[i]) for i, (a, b, c) in enumerate(steps)]
+    outs = [pltpu.make_async_copy(b, c, outsem.at[i]) for i, (a, b, c) in enumerate(steps)]
+    for copy in ins:
+        copy.start()
+    for load, store in zip(ins, outs):
+        load.wait()
+        store.start()
+    for copy in outs:
+        copy.wait()
 
 
 def solution(mesh):
@@ -478,7 +493,7 @@
         vm = pltpu.VMEM
         dma = pltpu.SemaphoreType.DMA
         row = (batch, tile_c)
-        return pl.pallas_call(
+        xd, xp = pl.pallas_call(
             functools.partial(kernel, nrows, ncols, lat_rows, lat_cols),
             out_shape=(
                 jax.ShapeDtypeStruct(die_current.shape, F32),
@@ -539,6 +554,22 @@
                 collective_id=0, has_side_effects=True, vmem_limit_bytes=67043328
             ),
         )(die_current, die_shunt, pkg_current, pkg_matrix, pkg_block_inv, nodes, cond)
+        return pl.pallas_call(
+            deliver,
+            out_shape=(
+                jax.ShapeDtypeStruct(xd.shape, F32),
+                jax.ShapeDtypeStruct(xp.shape, F32),
+            ),
+            in_specs=[pl.BlockSpec(memory_space=pltpu.HBM)] * 2,
+            out_specs=(pl.BlockSpec(memory_space=pltpu.HBM),) * 2,
+            scratch_shapes=[
+                vm(xd.shape, F32),
+                vm(xp.shape, F32),
+                dma((batch + 1,)),
+                dma((batch + 1,)),
+            ],
+            compiler_params=pltpu.CompilerParams(vmem_limit_bytes=67043328),
+        )(xd, xp)
 
     placed = (
         P(None, "row", "col"),

time: 46.2 us -> 43.6 us (0.944)
  local copies, waits for them, and re-layouts: 3.7 us -> 0 us
  Pallas kernels: 41.7 us -> 42.7 us
    unnamed x4 -> x0, local copies, waits for them, and re-layouts: 3.7 us -> none
    pallas_call x0 -> x1, Pallas kernels: none -> 2.59 us  [body(): pl.pallas_call(deliver, out_shape=(jax.ShapeDtypeStruct(xd.shape, F32), j...]
    pallas_call x1, Pallas kernels: 41.7 us -> 40.1 us  [body(): pl.pallas_call(functools.partial(kernel, nrows, ncols, lat_rows, lat_cols...]
where the time goes in v5:
time: 43.6 us; the launch traced here: 43.4 us
  Pallas kernels  42.7 us (98%)
  between operations  0.64 us (1%)
    pallas_call x1, Pallas kernels, body(): pl.pallas_call(functools.partial(kernel, nrows, ncols, lat_rows, lat_cols...  40.1 us
    pallas_call x1, Pallas kernels, body(): pl.pallas_call(deliver, out_shape=(jax.ShapeDtypeStruct(xd.shape, F32), j...  2.59 us

profile of v5, /device:TPU:0, one launch (start us, length us, event | category | flops | bytes accessed | tf_op | source)
XLA Modules:
  0.0 43.4 jit_solution(10433488301729616898)
XLA Ops:
  0.6 40.1 %shard_map.86 = (f32[16,128,256]{2,1,0:T(8,128)}, f32[16,128]{1,0:T(8,128)}) custom-call(f32[16,128,256]{2,1,0:T(8,128)} %rd_hbm.1, f32[128,256]{1,0:T(8,128)} %shunt_hbm.1, f32[16,128]{1,0:T(8,128)} %rp_hbm.1, f32[512,1024]{1,0:T(8,128)} %mat_hbm.1, f32[4,32,32]{2,1,0:T(8,128)} %inv_hbm.1, s32[32,128]{1,0:T(8,128)} %bitcast.2, f32[32,128]{1,0:T(8,128)} %bitcast.3), custom_call_target="tpu_custom_call" | custom-call | tf_op jit(solution)/shard_map/pallas_call | solution.py:496
  40.8 2.6 %shard_map.87 = (f32[16,128,256]{2,1,0:T(8,128)}, f32[16,128]{1,0:T(8,128)}) custom-call(f32[16,128,256]{2,1,0:T(8,128)} %get-tuple-element.4.x_hbm, f32[16,128]{1,0:T(8,128)} %get-tuple-element.5.p_hbm), custom_call_target="tpu_custom_call" | custom-call | tf_op jit(solution)/shard_map/pallas_call | solution.py:557
